TPU v7x, 32 devices: a whole 2x2x4 slice. The times are simulated.
32 devices in a mesh: seq: 4 (over x, core), exp: 8 (over z, y).
Axes of the slice: x: 2, y: 2, z: 4, core: 2. Of those that a mesh axis runs over, the one named last changes fastest.
Arguments:
- residual_in: bfloat16 [4096, 2048], P(('seq', 'exp')), may hold values from -8 to 8
- ssm_input: bfloat16 [4096, 2048], P(('seq', 'exp')), may hold values from -6 to 6
- ssm_b: bfloat16 [4096, 128], P(('seq', 'exp')), may hold values from -6 to 6
- ssm_c: bfloat16 [4096, 128], P(('seq', 'exp')), may hold values from -0.5 to 0.5
- log_decay: float32 [4096, 32], P(('seq', 'exp')), may hold values from -2 to 0, as said below
- skip_gain: float32 [32], replicated, may hold values from 0.5 to 1.5
- out_proj: bfloat16 [2048, 2048], replicated, may hold values from -0.125 to 0.125
- norm_gain: float32 [2048], replicated, may hold values from 0.5 to 1.5
- router: bfloat16 [2048, 16], replicated, may hold values from -1 to 1
- assignment: int32 [4096, 1], P(('seq', 'exp')), may hold values from 0 to 15; in each aligned block of 128 rows (0 to 127, 128 to 255, ...) at most 16 rows name the same one
- expert_gate: bfloat16 [32, 2048, 704], P(('seq', 'exp')), may hold values from -0.125 to 0.125
- expert_up: bfloat16 [32, 2048, 704], P(('seq', 'exp')), may hold values from -0.125 to 0.125
- expert_down: bfloat16 [32, 704, 2048], P(('seq', 'exp')), may hold values from -0.15625 to 0.15625
Outputs:
- layer_out: bfloat16 [4096, 2048], P(('seq', 'exp'))
- route_weight: float32 [4096], P(('seq', 'exp'))
Inputs may be any that keep to these rules, and one draw needn't show every extreme that they name: `log_decay`: every entry is negative. `assignment`: on the rows of one device no expert is named more than 16 times; in every draw some expert is named exactly 16 times on some device.
All inputs are finite; a program needn't handle non-finite values.
Results may differ from a plain program's by a relative error of at most 0.009.
Values may be sent and summed in bfloat16 or wider, within the bound.
A program may use at most 576 MiB of HBM per device.

v0:
```python
import jax
import jax.numpy as jnp
from jax import lax
from jax.sharding import PartitionSpec as P

BLOCK = 128
SINK_ITERS = 8


def entering(x, axis, combine, identity):
    devices, here = (lax.axis_size(axis), lax.axis_index(axis))
    everything = jax.tree.map(lambda part: lax.all_gather(part, axis), x)
    start = jax.tree.map(
        lambda part, zero: jnp.broadcast_to(jnp.asarray(zero, part.dtype), part.shape), x, identity
    )

    def turn(k, before):
        reached = k < here
        new = combine(before, jax.tree.map(lambda part: part[k], everything))
        return jax.tree.map(lambda a, b: jnp.where(reached, a, b), new, before)

    return lax.fori_loop(0, devices, turn, start)


def widen(per_head, width):
    return jnp.repeat(per_head, width // per_head.shape[-1], axis=-1)


def block_terms(values, b_blocks, c_blocks, decay):
    block_count, length, head_count, head_size = values.shape
    cumulative = jnp.cumsum(decay, axis=1)
    weight = jnp.sqrt(-jnp.expm1(2.0 * decay))
    scores = jnp.einsum("ktn,ksn->kts", c_blocks, b_blocks, preferred_element_type=jnp.float32)
    leading = jnp.swapaxes(cumulative, 1, 2)
    distance = leading[:, :, :, None] - leading[:, :, None, :]
    causal = jnp.arange(length)[:, None] >= jnp.arange(length)[None, :]
    decay_mix = jnp.where(causal, jnp.exp(jnp.minimum(distance, 0.0)), 0.0) * (
        jnp.swapaxes(weight, 1, 2)[:, :, None, :] * scores[:, None, :, :]
    )
    decay_mix = decay_mix.astype(jnp.bfloat16)
    inner_part = jnp.einsum(
        "khts,kshp->kthp", decay_mix, values, preferred_element_type=jnp.float32
    )
    inner_part = inner_part.reshape(block_count, length, head_count * head_size)
    tail_weight = jnp.exp(cumulative[:, -1:, :] - cumulative) * weight
    row_width = head_count * head_size
    flat_values = values.reshape(block_count, length, row_width)
    tail_in = (flat_values.astype(jnp.float32) * widen(tail_weight, row_width)).astype(jnp.bfloat16)
    block_state = jnp.einsum("ksn,ksc->knc", b_blocks, tail_in, preferred_element_type=jnp.float32)
    return (inner_part, cumulative, block_state)


def combine_states(earlier, following):
    factor = widen(jnp.exp(following[0]), earlier[1].shape[1])
    return (earlier[0] + following[0], factor[None, :] * earlier[1] + following[1])


def local_step(entry, pieces):
    total, state = pieces
    return (widen(jnp.exp(total), entry.shape[1])[None, :] * entry + state, entry)


def balance(kernel, chosen_hot):
    column = jnp.ones((kernel.shape[1],), jnp.float32)
    for sweep in range(SINK_ITERS):
        row_scale = 1.0 / jnp.sum(kernel * column[None, :], axis=1)
        column = 1.0 / lax.psum(jnp.sum(kernel * row_scale[:, None], axis=0), ("seq", "exp"))
    weighted = kernel * column[None, :]
    return (
        kernel.shape[1]
        * jnp.sum(jnp.where(chosen_hot, weighted, 0.0), axis=1)
        / jnp.sum(weighted, axis=1)
    )


def feed_forward(arrived, gate_full, up_full, down_full):
    sources, slots, model_width = arrived.shape
    flat = arrived.reshape(sources * slots, model_width)
    gate_val = jnp.dot(flat, gate_full, preferred_element_type=jnp.float32)
    up_val = jnp.dot(flat, up_full, preferred_element_type=jnp.float32)
    hidden = (jax.nn.silu(gate_val) * up_val).astype(jnp.bfloat16)
    return jnp.dot(hidden, down_full, preferred_element_type=jnp.float32).reshape(
        sources, slots, model_width
    )


def per_device(
    residual_in,
    ssm_input,
    ssm_b,
    ssm_c,
    log_decay,
    skip_gain,
    out_proj,
    norm_gain,
    router,
    assignment,
    expert_gate,
    expert_up,
    expert_down,
):
    head_count = skip_gain.shape[0]
    length, row_width = ssm_input.shape
    head_size = row_width // head_count
    state_size = ssm_b.shape[1]
    model_width = residual_in.shape[1]
    block_count = length // BLOCK
    values = ssm_input.reshape(block_count, BLOCK, head_count, head_size)
    b_blocks = ssm_b.reshape(block_count, BLOCK, state_size)
    c_blocks = ssm_c.reshape(block_count, BLOCK, state_size)
    decay = log_decay.reshape(block_count, BLOCK, head_count)
    inner_part, cumulative, block_state = block_terms(values, b_blocks, c_blocks, decay)
    block_total = cumulative[:, -1, :]
    device_state, local_entry = lax.scan(
        local_step, jnp.zeros_like(block_state[0]), (block_total, block_state)
    )
    prefix_log = jnp.cumsum(block_total, axis=0) - block_total
    device_log = jnp.sum(block_total, axis=0)
    identity = (jnp.zeros((head_count,), jnp.float32), jnp.zeros_like(device_state))
    earlier_log, carried_in = entering(
        (device_log, device_state), ("seq", "exp"), combine_states, identity
    )
    entry = widen(jnp.exp(prefix_log), row_width)[:, None, :] * carried_in[None] + local_entry
    entry_rounded = entry.astype(jnp.bfloat16)
    carried = widen(jnp.exp(cumulative), row_width) * jnp.einsum(
        "ktn,knc->ktc", c_blocks, entry_rounded, preferred_element_type=jnp.float32
    )
    skip_wide = widen(skip_gain, row_width)
    flat_values = ssm_input.reshape(block_count, BLOCK, row_width).astype(jnp.float32)
    scan_out = (
        (inner_part + carried + skip_wide[None, None, :] * flat_values)
        .reshape(length, row_width)
        .astype(jnp.bfloat16)
    )
    mixed = residual_in.astype(jnp.float32) + jnp.dot(
        scan_out, out_proj, preferred_element_type=jnp.float32
    )
    scale = lax.rsqrt(jnp.mean(mixed * mixed, axis=1, keepdims=True) + 1e-05)
    normed = (mixed * scale * norm_gain[None, :]).astype(jnp.bfloat16)
    kernel = jnp.exp(jnp.dot(normed, router, preferred_element_type=jnp.float32))
    experts = router.shape[1]
    capacity = 2 * length // experts
    chosen = assignment[:, 0]
    chosen_hot = chosen[:, None] == jnp.arange(experts, dtype=jnp.int32)[None, :]
    route_weight = balance(kernel, chosen_hot)
    hot_int = chosen_hot.astype(jnp.int32)
    slot = jnp.sum(jnp.cumsum(hot_int, axis=0) * hot_int, axis=1) - 1
    position = chosen * capacity + slot
    packed = jnp.zeros((experts * capacity, model_width), jnp.bfloat16).at[position].set(normed)
    doubled = jnp.broadcast_to(
        packed.reshape(experts, 1, capacity, model_width), (experts, 2, capacity, model_width)
    )
    doubled = doubled.reshape(2 * experts, capacity, model_width)
    partial_value = feed_forward(
        lax.all_to_all(doubled, ("seq", "exp"), split_axis=0, concat_axis=0, tiled=True),
        expert_gate[0],
        expert_up[0],
        expert_down[0],
    )
    returned = lax.all_to_all(
        partial_value.astype(jnp.bfloat16), ("seq", "exp"), split_axis=0, concat_axis=0, tiled=True
    ).astype(partial_value.dtype)
    summed = jnp.sum(returned.reshape(experts, 2, capacity, model_width), axis=1).astype(
        jnp.bfloat16
    )
    summed = summed.reshape(experts * capacity, model_width)
    expert_out = summed[position]
    layer_out = (mixed + route_weight[:, None] * expert_out.astype(jnp.float32)).astype(
        jnp.bfloat16
    )
    return (layer_out, route_weight)


def solution(mesh):
    in_specs = (
        P(("seq", "exp"), None),
        P(("seq", "exp"), None),
        P(("seq", "exp"), None),
        P(("seq", "exp"), None),
        P(("seq", "exp"), None),
        P(),
        P(),
        P(),
        P(),
        P(("seq", "exp"), None),
        P(("seq", "exp"), None, None),
        P(("seq", "exp"), None, None),
        P(("seq", "exp"), None, None),
    )
    out_specs = (P(("seq", "exp"), None), P(("seq", "exp")))
    return jax.shard_map(
        per_device, mesh=mesh, in_specs=in_specs, out_specs=out_specs, check_vma=False
    )
```

profile of v0, /device:TPU:1, one launch (start us, length us, event | category | flops | bytes accessed | tf_op | source)
XLA Modules:
  0.0 760.8 jit_solution(15610699507661942850)
XLA Ops:
  19.5 61.6 %all-gather = f32[32,1,32]{2,1,0:T(1,128)S(1)} all-gather(f32[1,1,32]{2,1,0:T(1,128)} %get-tuple-element.165), channel_id=2, replica_groups=mesh['seq'=4,'exp'=8] {'seq','exp'}, dimensions={0}, use_global_device_ids=true | all-gather | bytes 4224 | tf_op jit(solution)/shard_map/all_gather | solution.py:12
  86.1 116.6 %all-gather.4.cloned.1.call-done = f32[4096,2048]{0,1:T(8,128)} async-done(((f32[128,2048]{0,1:T(8,128)}), f32[4096,2048]{0,1:T(8,128)}) %all-gather.4.cloned.1.call-update) | async-done | bytes 33554448 | tf_op jit(solution)/shard_map/all_gather | solution.py:12
  202.7 33.4 %copy.62 = f32[4096,2048]{1,0:T(8,128)} copy(f32[4096,2048]{0,1:T(8,128)} %all-gather.4.cloned.1.call-done) | data formatting | bytes 67108864
  236.1 92.5 %while.9 = (s32[]{:T(128)}, f32[128,2048]{1,0:T(8,128)}, s32[]{:T(128)}, f32[32,32]{1,0:T(8,128)S(1)}, f32[32,128,2048]{2,1,0:T(8,128)}, /*index=5*/s32[]{:T(128)}, s32[]{:T(128)}) while((s32[]{:T(128)}, f32[128,2048]{1,0:T(8,128)}, s32[]{:T(128)}, f32[32,32]{1,0:T(8,128)S(1)}, f32[32,128,2048]{2,1,0:T(8,128)}, ...), condition=%wide.region_2.3_spmd.clone, body=%wide.region_1.2_spmd.clone.sunk | while | flops 1048580 | bytes 3178985 | solution.py:22
  238.9 2.7 fusion.50
  244.7 2.7 fusion.50
  329.7 7.1 multiply_reduce_fusion
  336.8 3.2 scatter_custom_fusion
  340.1 2.8 broadcast_in_dim.94
  342.8 6.0 all-to-all-start
  350.5 66.0 %psum.56 = f32[16]{0:T(128)S(1)} all-reduce(f32[16]{0:T(128)S(1)} %multiply_reduce_fusion.15), channel_id=1, replica_groups=mesh['seq'=4,'exp'=8] {'seq','exp'}, use_global_device_ids=true, to_apply=%region_6.7 | all-reduce | flops 16 | bytes 128 | tf_op jit(solution)/shard_map/psum | solution.py:67
  416.7 38.7 %psum.57 = f32[16]{0:T(128)S(1)} all-reduce(f32[16]{0:T(128)S(1)} %multiply_reduce_fusion.13), channel_id=1, replica_groups=mesh['seq'=4,'exp'=8] {'seq','exp'}, use_global_device_ids=true, to_apply=%region_9.10 | all-reduce | flops 16 | bytes 128 | tf_op jit(solution)/shard_map/psum | solution.py:67
  455.6 4.3 fusion.4
  459.9 4.3 fusion.14
  466.5 4.2 convolution_convert_fusion
  470.7 7.1 all-to-all-start.1
  477.9 67.6 %psum.58 = f32[16]{0:T(128)S(1)} all-reduce(f32[16]{0:T(128)S(1)} %multiply_reduce_fusion.11), channel_id=1, replica_groups=mesh['seq'=4,'exp'=8] {'seq','exp'}, use_global_device_ids=true, to_apply=%region_12.13 | all-reduce | flops 16 | bytes 128 | tf_op jit(solution)/shard_map/psum | solution.py:67
  545.7 38.5 %psum.59 = f32[16]{0:T(128)S(1)} all-reduce(f32[16]{0:T(128)S(1)} %multiply_reduce_fusion.9), channel_id=1, replica_groups=mesh['seq'=4,'exp'=8] {'seq','exp'}, use_global_device_ids=true, to_apply=%region_15.16 | all-reduce | flops 16 | bytes 128 | tf_op jit(solution)/shard_map/psum | solution.py:67
  584.5 41.5 %psum.60 = f32[16]{0:T(128)S(1)} all-reduce(f32[16]{0:T(128)S(1)} %multiply_reduce_fusion.7), channel_id=1, replica_groups=mesh['seq'=4,'exp'=8] {'seq','exp'}, use_global_device_ids=true, to_apply=%region_18.19 | all-reduce | flops 16 | bytes 128 | tf_op jit(solution)/shard_map/psum | solution.py:67
  626.2 38.5 %psum.61 = f32[16]{0:T(128)S(1)} all-reduce(f32[16]{0:T(128)S(1)} %multiply_reduce_fusion.5), channel_id=1, replica_groups=mesh['seq'=4,'exp'=8] {'seq','exp'}, use_global_device_ids=true, to_apply=%region_21.22 | all-reduce | flops 16 | bytes 128 | tf_op jit(solution)/shard_map/psum | solution.py:67
  665.0 41.5 %psum.62 = f32[16]{0:T(128)S(1)} all-reduce(f32[16]{0:T(128)S(1)} %multiply_reduce_fusion.3), channel_id=1, replica_groups=mesh['seq'=4,'exp'=8] {'seq','exp'}, use_global_device_ids=true, to_apply=%region_24.25 | all-reduce | flops 16 | bytes 128 | tf_op jit(solution)/shard_map/psum | solution.py:67
  706.7 38.7 %psum.63 = f32[16]{0:T(128)S(1)} all-reduce(f32[16]{0:T(128)S(1)} %multiply_reduce_fusion.1), channel_id=1, replica_groups=mesh['seq'=4,'exp'=8] {'seq','exp'}, use_global_device_ids=true, to_apply=%region_27.28 | all-reduce | flops 16 | bytes 128 | tf_op jit(solution)/shard_map/psum | solution.py:67
  745.6 3.3 bitcast_reduce_fusion
  748.9 2.8 gather_fusion
  (215 shorter events, 113.1 us)
Async XLA Ops:
  7.2 459.3 %copy-start = (bf16[1,704,2048]{2,1,0:T(8,128)(2,1)S(1)}, bf16[1,704,2048]{2,1,0:T(8,128)(2,1)}, u32[]{:S(2)}) copy-start(bf16[1,704,2048]{2,1,0:T(8,128)(2,1)} %param.27) | copy-start | bytes 8650756
  7.2 5.9 copy-start.2
  7.2 195.5 %all-gather.4.cloned.1.call-start = ((), (), s32[]{:S(2)}) async-start(), calls=%async_computation.2 | async-start | bytes 34603008 | tf_op jit(solution)/shard_map/all_gather | solution.py:12
  236.1 93.6 %copy-start.1 = (bf16[128,128]{1,0:T(8,128)(2,1)S(1)}, bf16[128,128]{1,0:T(8,128)(2,1)}, u32[]{:S(2)}) copy-start(bf16[128,128]{1,0:T(8,128)(2,1)} %param.18) | copy-start | bytes 98308
  236.1 93.6 %copy-start.5 = (f32[2048]{0:T(1024)S(1)}, f32[2048]{0:T(1024)}, u32[]{:S(2)}) copy-start(f32[2048]{0:T(1024)} %broadcast_in_dim.48) | copy-start | bytes 24580
  236.1 93.6 %copy-start.6 = (f32[2048]{0:T(1024)S(1)}, f32[2048]{0:T(1024)}, u32[]{:S(2)}) copy-start(f32[2048]{0:T(1024)} %mul.305) | copy-start | bytes 24580
  329.7 7.1 copy-start.4
  342.8 6.0 copy-start.3
  342.8 112.7 %all-to-all-start = ((bf16[32,16,2048]{2,1,0:T(8,128)(2,1)}), bf16[32,16,2048]{2,1,0:T(8,128)(2,1)}, u32[]{:S(2)}, u32[]{:S(2)}) async-start(bf16[32,16,2048]{2,1,0:T(8,128)(2,1)} %bitcast.101), calls=%async_computation | async-start | bytes 4194304 | tf_op jit(solution)/shard_map/all_to_all | solution.py:155
  455.6 4.3 copy-start.9
  470.7 274.8 %copy-start.7 = (s32[128,1]{0,1:T(1,128)S(1)}, s32[128,1]{0,1:T(1,128)}, u32[]{:S(2)}) copy-start(s32[128,1]{0,1:T(1,128)} %param.24) | copy-start | bytes 1540
  470.7 274.9 %all-to-all-start.1 = ((bf16[32,16,2048]{2,1,0:T(8,128)(2,1)}), bf16[32,16,2048]{2,1,0:T(8,128)(2,1)}, u32[]{:S(2)}, u32[]{:S(2)}) async-start(bf16[32,16,2048]{2,1,0:T(8,128)(2,1)} %convolution_convert_fusion), calls=%async_computation.1 | async-start | bytes 4194304 | tf_op jit(solution)/shard_map/all_to_all | solution.py:160
  745.6 6.2 copy-start.8
Sparse Core Ops, SparseCore 0:
  15.2 187.4 all-gather.3
where the time goes:
time: 765 us; the launch traced here: 761 us
  blocking collectives  433 us (57%)
  waiting for transfers between devices  117 us (15%)
  other arithmetic  102 us (13%)
  local copies, waits for them, and re-layouts  54.4 us (7%)
  matrix products  27.2 us (4%)
  between operations  14.3 us (2%)
  starting transfers between devices  13.2 us (2%)
    psum x8, blocking collectives, balance(): lax.psum(jnp.sum(kernel * row_scale[:, None], axis=0), ('seq', 'exp'))  371 us
    all_gather x1, waiting for transfers between devices, entering(): everything = jax.tree.map(lambda part: lax.all_gather(part, axis), x)  117 us
    select_n x32, other arithmetic, turn(): return jax.tree.map(lambda a, b: jnp.where(reached, a, b), new, before)  87.5 us
    all_gather x1, blocking collectives, entering(): everything = jax.tree.map(lambda part: lax.all_gather(part, axis), x)  61.6 us
    unnamed x22, local copies, waits for them, and re-layouts  34.7 us
  transfers between devices with their start and end apart: 3, of which 1 were waited for; matrix products, arithmetic and copies ran while one was open for 2% of the time, Pallas kernels for 0%

commit v1 on v0

v1 whole, which is shorter than its diff:
```python
import functools

import jax
import jax.numpy as jnp
from jax import lax
from jax.experimental import pallas as pl
from jax.experimental.pallas import tpu as pltpu
from jax.sharding import PartitionSpec as P

SINK_ITERS = 8
LANES = 128
TOTAL_ROWS = 16
MESH = pl.DeviceIdType.MESH


def place(flat):
    across = lax.axis_size("exp")
    return (flat // across, flat % across)


def own_index():
    return lax.axis_index("seq") * lax.axis_size("exp") + lax.axis_index("exp")


def device_count():
    return lax.axis_size("seq") * lax.axis_size("exp")


def meet_all(me, devices):
    barrier = pltpu.get_barrier_semaphore()

    @pl.loop(1, devices)
    def _(step):
        pl.semaphore_signal(
            barrier, inc=1, device_id=place((me + step) % devices), device_id_type=MESH
        )

    pl.semaphore_wait(barrier, devices - 1)


def entry_kernel(devices, src_ref, out_ref, arrived, entries, go_send, go_recv, back_send, back_recv, own_sem):
    me = own_index()
    groups = out_ref.shape[1] // LANES
    rows = entries.shape[1]

    def part_of(flat):
        return src_ref.at[flat // groups, :, pl.ds(pl.multiple_of((flat % groups) * LANES, LANES), LANES)]

    def region_of(flat):
        return out_ref.at[
            pl.ds(pl.multiple_of((flat // groups) * rows, rows), rows),
            pl.ds(pl.multiple_of((flat % groups) * LANES, LANES), LANES),
        ]

    def outgoing(peer):
        return pltpu.make_async_remote_copy(
            src_ref=part_of(peer), dst_ref=arrived.at[me], send_sem=go_send.at[peer],
            recv_sem=go_recv.at[me], device_id=place(peer), device_id_type=MESH)

    def incoming(peer):
        return pltpu.make_async_remote_copy(
            src_ref=part_of(peer), dst_ref=arrived.at[peer], send_sem=go_send.at[peer],
            recv_sem=go_recv.at[peer], device_id=place(peer), device_id_type=MESH)

    def returning(peer):
        return pltpu.make_async_remote_copy(
            src_ref=entries.at[peer], dst_ref=region_of(me), send_sem=back_send.at[peer],
            recv_sem=back_recv.at[me], device_id=place(peer), device_id_type=MESH)

    def returned(peer):
        return pltpu.make_async_remote_copy(
            src_ref=entries.at[peer], dst_ref=region_of(peer), send_sem=back_send.at[peer],
            recv_sem=back_recv.at[peer], device_id=place(peer), device_id_type=MESH)

    own = pltpu.make_async_copy(part_of(me), arrived.at[me], own_sem)
    own.start()
    meet_all(me, devices)

    @pl.loop(1, devices)
    def _(step):
        outgoing((me + step) % devices).start()

    own.wait()

    @pl.loop(1, devices)
    def _(step):
        incoming((me + devices - step) % devices).wait_recv()

    def advance(k, state):
        entries[k] = state.astype(entries.dtype)
        block = arrived[k]
        total = jnp.sum(block[rows:rows + TOTAL_ROWS].astype(jnp.float32), axis=0, keepdims=True)
        return jnp.exp(total) * state + block[:rows].astype(jnp.float32)

    lax.fori_loop(0, devices, advance, jnp.zeros((rows, LANES), jnp.float32))

    @pl.loop(1, devices)
    def _(step):
        returning((me + step) % devices).start()

    own_back = pltpu.make_async_copy(entries.at[me], region_of(me), own_sem)
    own_back.start()

    @pl.loop(1, devices)
    def _(step):
        peer = (me + devices - step) % devices
        returned(peer).wait_recv()
        outgoing(peer).wait_send()
        returning(peer).wait_send()

    own_back.wait()


def entering(block_state, total):
    devices = device_count()
    state_size, width = block_state.shape
    parts = devices // (width // LANES)
    rows = state_size // parts
    high = total.astype(jnp.bfloat16)
    low = (total - high.astype(jnp.float32)).astype(jnp.bfloat16)
    totals = jnp.concatenate(
        [high[None], low[None], jnp.zeros((TOTAL_ROWS - 2, width), jnp.bfloat16)], axis=0
    )
    sent = jnp.concatenate(
        [
            block_state.astype(jnp.bfloat16).reshape(parts, rows, width),
            jnp.broadcast_to(totals[None], (parts, TOTAL_ROWS, width)),
        ],
        axis=1,
    )
    dma = pltpu.SemaphoreType.DMA
    return pl.pallas_call(
        functools.partial(entry_kernel, devices),
        out_shape=jax.ShapeDtypeStruct((state_size, width), jnp.bfloat16),
        in_specs=[pl.BlockSpec(memory_space=pltpu.VMEM)],
        out_specs=pl.BlockSpec(memory_space=pltpu.VMEM),
        scratch_shapes=[
            pltpu.VMEM((devices, rows + TOTAL_ROWS, LANES), jnp.bfloat16),
            pltpu.VMEM((devices, rows, LANES), jnp.bfloat16),
            dma((devices,)), dma((devices,)), dma((devices,)), dma((devices,)), dma,
        ],
        compiler_params=pltpu.CompilerParams(collective_id=0, has_side_effects=True),
        name="entry_states",
    )(sent)


def dispatch_kernel(devices, packed_ref, kernel_ref, rows_ref, table_ref,
                    go_send, go_recv, pass_send, pass_recv, table_send, table_recv, own_sem):
    me = own_index()
    side, mine = me % 2, me // 2
    experts = devices // 2
    partner = me + 1 - 2 * side

    def table_copy(peer, slot):
        return pltpu.make_async_remote_copy(
            src_ref=kernel_ref, dst_ref=table_ref.at[slot], send_sem=table_send.at[peer],
            recv_sem=table_recv.at[slot], device_id=place(peer), device_id_type=MESH)

    def row_copy(other, slot):
        return pltpu.make_async_remote_copy(
            src_ref=packed_ref.at[other], dst_ref=rows_ref.at[side, slot], send_sem=go_send.at[other],
            recv_sem=go_recv.at[slot], device_id=place(2 * other + side), device_id_type=MESH)

    def pass_copy(at, slot):
        return pltpu.make_async_remote_copy(
            src_ref=rows_ref.at[side, slot], dst_ref=rows_ref.at[at, slot], send_sem=pass_send.at[slot],
            recv_sem=pass_recv.at[slot], device_id=place(partner), device_id_type=MESH)

    own_rows = pltpu.make_async_copy(packed_ref.at[mine], rows_ref.at[side, mine], own_sem.at[0])
    own_table = pltpu.make_async_copy(kernel_ref, table_ref.at[me], own_sem.at[1])
    own_rows.start()
    own_table.start()
    meet_all(me, devices)

    @pl.loop(1, devices)
    def _(step):
        table_copy((me + step) % devices, me).start()

    @pl.loop(1, experts)
    def _(step):
        row_copy((mine + step) % experts, mine).start()

    own_rows.wait()
    pass_copy(side, mine).start()

    @pl.loop(1, experts)
    def _(step):
        source = (mine + experts - step) % experts
        row_copy(source, source).wait_recv()
        pass_copy(side, source).start()

    own_table.wait()

    @pl.loop(1, devices)
    def _(step):
        peer = (me + devices - step) % devices
        table_copy(peer, peer).wait_recv()
        table_copy(peer, peer).wait_send()

    @pl.loop(0, experts)
    def _(step):
        source = (mine + experts - step) % experts
        pass_copy(1 - side, source).wait_recv()
        pass_copy(side, source).wait_send()

    @pl.loop(1, experts)
    def _(step):
        other = (mine + step) % experts
        row_copy(other, other).wait_send()


def dispatch(packed, kernel):
    devices = device_count()
    experts, capacity, width = packed.shape
    dma = pltpu.SemaphoreType.DMA
    vmem = pl.BlockSpec(memory_space=pltpu.VMEM)
    return pl.pallas_call(
        functools.partial(dispatch_kernel, devices),
        out_shape=(
            jax.ShapeDtypeStruct((2, experts, capacity, width), packed.dtype),
            jax.ShapeDtypeStruct((devices, *kernel.shape), kernel.dtype),
        ),
        in_specs=[vmem, vmem],
        out_specs=(vmem, vmem),
        scratch_shapes=[
            dma((experts,)), dma((experts,)), dma((experts,)), dma((experts,)),
            dma((devices,)), dma((devices,)), dma((2,)),
        ],
        compiler_params=pltpu.CompilerParams(collective_id=1, has_side_effects=True),
        name="dispatch_rows",
    )(packed, kernel)


def collect_kernel(devices, half_ref, out_ref, partial, summed,
                   swap_send, swap_recv, back_send, back_recv, own_sem):
    me = own_index()
    side, mine = me % 2, me // 2
    experts = devices // 2
    partner = me + 1 - 2 * side

    def swap_copy(slot):
        return pltpu.make_async_remote_copy(
            src_ref=half_ref.at[1 - side, slot], dst_ref=partial.at[slot], send_sem=swap_send.at[slot],
            recv_sem=swap_recv.at[slot], device_id=place(partner), device_id_type=MESH)

    def back_copy(other, slot):
        return pltpu.make_async_remote_copy(
            src_ref=summed.at[other], dst_ref=out_ref.at[slot], send_sem=back_send.at[other],
            recv_sem=back_recv.at[slot], device_id=place(2 * other + side), device_id_type=MESH)

    def add_up(slot):
        swap_copy(slot).wait_recv()
        summed[slot] = (
            half_ref[side, slot].astype(jnp.float32) + partial[slot].astype(jnp.float32)
        ).astype(summed.dtype)

    barrier = pltpu.get_barrier_semaphore()

    @pl.loop(1, experts)
    def _(step):
        pl.semaphore_signal(
            barrier, inc=1, device_id=place(2 * ((mine + step) % experts) + side), device_id_type=MESH
        )

    pl.semaphore_signal(barrier, inc=1, device_id=place(partner), device_id_type=MESH)
    pl.semaphore_wait(barrier, experts)

    @pl.loop(1, experts + 1)
    def _(step):
        swap_copy((mine + step) % experts).start()

    @pl.loop(1, experts)
    def _(step):
        other = (mine + step) % experts
        add_up(other)
        back_copy(other, mine).start()

    add_up(mine)
    own = pltpu.make_async_copy(summed.at[mine], out_ref.at[mine], own_sem)
    own.start()

    @pl.loop(1, experts)
    def _(step):
        other = (mine + experts - step) % experts
        back_copy(other, other).wait_recv()
        back_copy(other, other).wait_send()

    @pl.loop(0, experts)
    def _(step):
        swap_copy(step).wait_send()

    own.wait()


def collect(halves):
    devices = device_count()
    _, experts, capacity, width = halves.shape
    dma = pltpu.SemaphoreType.DMA
    vmem = pl.BlockSpec(memory_space=pltpu.VMEM)
    block = pltpu.VMEM((experts, capacity, width), halves.dtype)
    return pl.pallas_call(
        functools.partial(collect_kernel, devices),
        out_shape=jax.ShapeDtypeStruct((experts, capacity, width), halves.dtype),
        in_specs=[vmem],
        out_specs=vmem,
        scratch_shapes=[
            block, block,
            dma((experts,)), dma((experts,)), dma((experts,)), dma((experts,)), dma,
        ],
        compiler_params=pltpu.CompilerParams(collective_id=2, has_side_effects=True),
        name="collect_rows",
    )(halves)


def balance_kernel(table_ref, own_ref, hot_ref, weight_ref):
    devices, experts, length = table_ref.shape
    some = 8

    def sweep(_, column):
        def add(k, totals):
            block = table_ref[pl.ds(pl.multiple_of(k * some, some), some)]
            row_scale = 1.0 / jnp.sum(block * column[None], axis=1, keepdims=True)
            return totals + jnp.sum(block * row_scale, axis=0)

        totals = lax.fori_loop(0, devices // some, add, jnp.zeros((experts, length), jnp.float32))
        return 1.0 / jnp.sum(totals, axis=1, keepdims=True)

    column = lax.fori_loop(0, SINK_ITERS, sweep, jnp.ones((experts, 1), jnp.float32))
    weighted = own_ref[...] * column
    picked = jnp.sum(jnp.where(hot_ref[...] > 0.0, weighted, 0.0), axis=0, keepdims=True)
    weight_ref[...] = experts * picked / jnp.sum(weighted, axis=0, keepdims=True)


def balance(table, own, hot):
    vmem = pl.BlockSpec(memory_space=pltpu.VMEM)
    return pl.pallas_call(
        balance_kernel,
        out_shape=jax.ShapeDtypeStruct((1, own.shape[1]), jnp.float32),
        in_specs=[vmem, vmem, vmem],
        out_specs=vmem,
        name="balance",
    )(table, own, hot)


def widen(per_head, width):
    return jnp.repeat(per_head, width // per_head.shape[-1], axis=-1)


def block_terms(values, b_matrix, c_matrix, decay):
    length, head_count, head_size = values.shape
    row_width = head_count * head_size
    cumulative = jnp.cumsum(decay, axis=0)
    weight = jnp.sqrt(-jnp.expm1(2.0 * decay))
    flat_values = values.reshape(length, row_width)
    tail_weight = jnp.exp(cumulative[-1:] - cumulative) * weight
    tail_in = (flat_values.astype(jnp.float32) * widen(tail_weight, row_width)).astype(jnp.bfloat16)
    block_state = jnp.einsum("sn,sc->nc", b_matrix, tail_in, preferred_element_type=jnp.float32)
    scores = jnp.einsum("tn,sn->ts", c_matrix, b_matrix, preferred_element_type=jnp.float32)
    leading = cumulative.T
    distance = leading[:, :, None] - leading[:, None, :]
    causal = jnp.arange(length)[:, None] >= jnp.arange(length)[None, :]
    decay_mix = jnp.where(causal, jnp.exp(jnp.minimum(distance, 0.0)), 0.0) * (
        weight.T[:, None, :] * scores[None, :, :]
    )
    decay_mix = decay_mix.astype(jnp.bfloat16)
    inner_part = jnp.einsum("hts,shp->thp", decay_mix, values, preferred_element_type=jnp.float32)
    return (inner_part.reshape(length, row_width), cumulative, block_state)


def feed_forward(flat, gate_half, up_half, down_half):
    gate_val = jnp.dot(flat, gate_half, preferred_element_type=jnp.float32)
    up_val = jnp.dot(flat, up_half, preferred_element_type=jnp.float32)
    hidden = (jax.nn.silu(gate_val) * up_val).astype(jnp.bfloat16)
    return jnp.dot(hidden, down_half, preferred_element_type=jnp.float32).astype(jnp.bfloat16)


def per_device(
    residual_in,
    ssm_input,
    ssm_b,
    ssm_c,
    log_decay,
    skip_gain,
    out_proj,
    norm_gain,
    router,
    assignment,
    expert_gate,
    expert_up,
    expert_down,
):
    head_count = skip_gain.shape[0]
    length, row_width = ssm_input.shape
    head_size = row_width // head_count
    model_width = residual_in.shape[1]
    values = ssm_input.reshape(length, head_count, head_size)
    inner_part, cumulative, block_state = block_terms(values, ssm_b, ssm_c, log_decay)
    entry_rounded = entering(block_state, widen(cumulative[-1], row_width))
    carried = widen(jnp.exp(cumulative), row_width) * jnp.dot(
        ssm_c, entry_rounded, preferred_element_type=jnp.float32
    )
    skip_wide = widen(skip_gain, row_width)
    scan_out = (inner_part + carried + skip_wide[None, :] * ssm_input.astype(jnp.float32)).astype(
        jnp.bfloat16
    )
    mixed = residual_in.astype(jnp.float32) + jnp.dot(
        scan_out, out_proj, preferred_element_type=jnp.float32
    )
    scale = lax.rsqrt(jnp.mean(mixed * mixed, axis=1, keepdims=True) + 1e-05)
    normed = (mixed * scale * norm_gain[None, :]).astype(jnp.bfloat16)
    kernel = jnp.exp(jnp.einsum("de,td->et", router, normed, preferred_element_type=jnp.float32))
    experts = router.shape[1]
    capacity = 2 * length // experts
    chosen = assignment[:, 0]
    hot = (chosen[:, None] == jnp.arange(experts, dtype=jnp.int32)[None, :]).astype(jnp.float32)
    upto = (jnp.arange(length)[:, None] >= jnp.arange(length)[None, :]).astype(jnp.bfloat16)
    counts = jnp.dot(upto, hot.astype(jnp.bfloat16), preferred_element_type=jnp.float32)
    slot = jnp.sum(counts * hot, axis=1).astype(jnp.int32) - 1
    position = chosen * capacity + slot
    spread = (
        position[:, None] == jnp.arange(experts * capacity, dtype=jnp.int32)[None, :]
    ).astype(jnp.bfloat16)
    packed = jnp.einsum("ts,td->sd", spread, normed, preferred_element_type=jnp.float32)
    packed = packed.astype(jnp.bfloat16).reshape(experts, capacity, model_width)
    arrived, table = dispatch(packed, kernel)
    route_weight = balance(table, kernel, hot.T)[0]
    halves = feed_forward(
        arrived.reshape(2 * experts * capacity, model_width),
        expert_gate[0],
        expert_up[0],
        expert_down[0],
    )
    summed = collect(halves.reshape(2, experts, capacity, model_width))
    expert_out = jnp.dot(
        spread, summed.reshape(experts * capacity, model_width), preferred_element_type=jnp.float32
    )
    layer_out = (mixed + route_weight[:, None] * expert_out).astype(jnp.bfloat16)
    return (layer_out, route_weight)


def solution(mesh):
    in_specs = (
        P(("seq", "exp"), None),
        P(("seq", "exp"), None),
        P(("seq", "exp"), None),
        P(("seq", "exp"), None),
        P(("seq", "exp"), None),
        P(),
        P(),
        P(),
        P(),
        P(("seq", "exp"), None),
        P(("seq", "exp"), None, None),
        P(("seq", "exp"), None, None),
        P(("seq", "exp"), None, None),
    )
    out_specs = (P(("seq", "exp"), None), P(("seq", "exp")))
    return jax.shard_map(
        per_device, mesh=mesh, in_specs=in_specs, out_specs=out_specs, check_vma=False
    )
```

time: 765 us -> 170 us (0.22)
  blocking collectives: 433 us -> 0 us
  Pallas kernels: 0 us -> 121 us
  waiting for transfers between devices: 117 us -> 0 us
  other arithmetic: 102 us -> 5.11 us
  local copies, waits for them, and re-layouts: 54.4 us -> 6.99 us
  between operations: 14.3 us -> 0.75 us
  starting transfers between devices: 13.2 us -> 0 us
    psum x8 -> x0, blocking collectives: 371 us -> none  [balance(): lax.psum(jnp.sum(kernel * row_scale[:, None], axis=0), ('seq', 'exp'))]
    pallas_call x0 -> x4, Pallas kernels: none -> 121 us  [the longest x1 44.5 us: dispatch(): pl.pallas_call(functools.partial(dispatch_kernel, devices), out_shape=(ja...]
    all_gather x1 -> x0, waiting for transfers between devices: 117 us -> none  [entering(): everything = jax.tree.map(lambda part: lax.all_gather(part, axis), x)]
    select_n x33 -> x0, other arithmetic: 88.2 us -> none  [the longest x32 87.5 us: turn(): return jax.tree.map(lambda a, b: jnp.where(reached, a, b), new, before)]
    all_gather x1 -> x0, blocking collectives: 61.6 us -> none  [entering(): everything = jax.tree.map(lambda part: lax.all_gather(part, axis), x)]
    unnamed x22 -> x16, local copies, waits for them, and re-layouts: 34.7 us -> 2.18 us
    all_to_all x2 -> x0, starting transfers between devices: 13.1 us -> none  [the longest x1 7.14 us: per_device(): lax.all_to_all(partial_value.astype(jnp.bfloat16), ('seq', 'exp'), split_...]
    dot_general x7 -> x9, matrix products: 20.1 us -> 27 us  [the longest x1 7.62 us: feed_forward(): jnp.dot(hidden, down_half, preferred_element_type=jnp.float32)]
  transfers between devices with their start and end apart: 3 -> 0, of which waited for: 1 -> 0; matrix products, arithmetic and copies ran while one was open for 2% -> 0% of each run, Pallas kernels for 0% -> 0%
where the time goes in v1:
time: 170 us; the launch traced here: 168 us
  Pallas kernels  121 us (71%)
  matrix products  33.9 us (20%)
  local copies, waits for them, and re-layouts  6.99 us (4%)
  other arithmetic  5.11 us (3%)
    pallas_call x1, Pallas kernels, dispatch(): pl.pallas_call(functools.partial(dispatch_kernel, devices), out_shape=(ja...  44.5 us
    pallas_call x1, Pallas kernels, entering(): pl.pallas_call(functools.partial(entry_kernel, devices), out_shape=jax.Sh...  38.8 us
    pallas_call x1, Pallas kernels, collect(): pl.pallas_call(functools.partial(collect_kernel, devices), out_shape=jax....  35 us
    dot_general x1, matrix products, feed_forward(): jnp.dot(hidden, down_half, preferred_element_type=jnp.float32)  7.62 us
    dot_general x1, matrix products, per_device(): jnp.dot(scan_out, out_proj, preferred_element_type=jnp.float32)  6.98 us
    dot_general x1, matrix products, feed_forward(): gate_val = jnp.dot(flat, gate_half, preferred_element_type=jnp.float32)  5.25 us

profile of v1, /device:TPU:1, one launch (start us, length us, event | category | flops | bytes accessed | tf_op | source)
XLA Modules:
  0.0 168.0 jit_solution(2758714705648368057)
XLA Ops:
  0.6 1.0 fusion.18
  1.6 1.2 fusion.36
  2.9 1.2 fusion.34.hot_ref
  4.1 0.7 broadcast_in_dim.24
  6.2 0.8 copy.22
  7.3 0.7 copy.23
  8.1 1.6 fusion.40
  9.7 0.7 copy.30
  11.1 1.3 copy.27
  12.5 0.8 fusion.20
  13.3 1.1 convolution_convert_fusion.2
  14.4 0.9 pad_maximum_fusion.src_ref
  15.3 38.8 %entry_states.1 = bf16[128,2048]{1,0:T(8,128)(2,1)} custom-call(bf16[2,80,2048]{2,1,0:T(8,128)(2,1)} %pad_maximum_fusion.src_ref), custom_call_target="tpu_custom_call" | custom-call | tf_op jit(solution)/shard_map/entry_states/pallas_call | solution.py:132
  54.1 2.8 %fusion.19 = f32[32,128,64]{1,2,0:T(8,128)} fusion(bf16[128,32,64]{0,2,1:T(8,128)(2,1)S(1)} %bitcast.70, f32[128,128]{1,0:T(8,128)} %fusion.40, f32[32,128]{1,0:T(8,128)} %copy.26, f32[32,128]{1,0:T(8,128)} %copy.23, pred[128,128]{1,0:T(8,128)(4,1)} %iota_compare_fusion.3), kind=kOutput, calls=%fused_computation.26 | convolution fusion | flops 70254592 | bytes 1687552 | tf_op jit(solution)/shard_map/hts,shp->thp/dot_general | solution.py:366
  56.9 1.1 broadcast_in_dim.19
  58.1 7.0 %multiply_reduce_fusion = (f32[128]{0:T(128)S(1)}, f32[128,2048]{1,0:T(8,128)}) fusion(bf16[2048,2048]{1,0:T(8,128)(2,1)} %param.19, f32[128,2048]{0,1:T(8,128)} %bitcast.76, f32[128,2048]{0,1:T(8,128)} %bitcast.72, bf16[128,2048]{1,0:T(8,128)(2,1)} %entry_states.1, bf16[128,128]{1,0:T(8,128)(2,1)S(1)} %copy-done.1, bf16[128,2048]{0,1:T(8,128)(2,1)S(1)} %copy.27, ...), kind=kOutput, calls=%fused_computation.29 | convolution fusion | flops 1143472000 | bytes 13148672 | tf_op jit(solution)/shard_map/dot_general | solution.py:406
  65.1 2.2 %fusion.17.kernel_ref.own_ref = f32[16,128]{1,0:T(8,128)} fusion(bf16[2048,16]{0,1:T(8,128)(2,1)S(1)} %copy-done.2, f32[128,2048]{1,0:T(8,128)} %get-tuple-element.12, f32[2048]{0:T(1024)S(1)} %copy-done.3, f32[128]{0:T(128)S(1)} %add_rsqrt_fusion), kind=kOutput, calls=%fused_computation.24 | convolution fusion | flops 9175040 | bytes 1131008 | tf_op jit(solution)/shard_map/de,td->et/dot_general | solution.py:411
  67.2 2.8 %convolution_convert_fusion.1 = bf16[256,2048]{1,0:T(8,128)(2,1)} fusion(s32[128]{0:T(128)S(1)} %copy-done.6, f32[128,2048]{1,0:T(8,128)} %get-tuple-element.12, f32[2048]{0:T(1024)S(1)} %copy-done.3, f32[128]{0:T(128)S(1)} %add_rsqrt_fusion), kind=kOutput, calls=%fused_computation.6 | convolution fusion | flops 135561216 | bytes 2106368 | tf_op jit(solution)/shard_map/ts,td->sd/dot_general | solution.py:423
  70.0 44.5 %dispatch_rows.1 = (bf16[2,16,16,2048]{3,2,1,0:T(8,128)(2,1)}, f32[32,16,128]{2,1,0:T(8,128)}) custom-call(bf16[16,16,2048]{2,1,0:T(8,128)(2,1)} %bitcast.73, f32[16,128]{1,0:T(8,128)} %fusion.17.kernel_ref.own_ref), custom_call_target="tpu_custom_call" | custom-call | tf_op jit(solution)/shard_map/dispatch_rows/pallas_call | solution.py:217
  114.5 3.0 %balance.1 = f32[1,128]{1,0:T(1,128)} custom-call(f32[32,16,128]{2,1,0:T(8,128)} %get-tuple-element.4.table_ref, f32[16,128]{1,0:T(8,128)} %fusion.17.kernel_ref.own_ref, f32[16,128]{1,0:T(8,128)} %fusion.34.hot_ref), custom_call_target="tpu_custom_call" | custom-call | tf_op jit(solution)/shard_map/balance/pallas_call | solution.py:336
  117.5 5.3 %fusion.3 = f32[512,704]{0,1:T(8,128)} fusion(bf16[512,2048]{1,0:T(8,128)(2,1)} %bitcast.82, bf16[1,2048,704]{1,2,0:T(8,128)(2,1)} %param.23), kind=kOutput, calls=%fused_computation.4 | convolution fusion | flops 1476395008 | bytes 6422528 | tf_op jit(solution)/shard_map/dot_general | solution.py:371
  122.7 7.6 %convolution_convert_fusion = bf16[512,2048]{1,0:T(8,128)(2,1)} fusion(bf16[1,704,2048]{2,1,0:T(8,128)(2,1)S(1)} %copy-done, bf16[512,2048]{1,0:T(8,128)(2,1)} %bitcast.83, bf16[1,2048,704]{1,2,0:T(8,128)(2,1)} %param.24, f32[512,704]{0,1:T(8,128)} %fusion.3), kind=kOutput, calls=%fused_computation | convolution fusion | flops 2956001280 | bytes 11403264 | tf_op jit(solution)/shard_map/dot_general | solution.py:374
  130.4 35.0 %collect_rows.1 = bf16[16,16,2048]{2,1,0:T(8,128)(2,1)} custom-call(bf16[2,16,16,2048]{3,2,1,0:T(8,128)(2,1)} %bitcast.74), custom_call_target="tpu_custom_call" | custom-call | tf_op jit(solution)/shard_map/collect_rows/pallas_call | solution.py:301
  165.3 2.7 %fusion.10 = bf16[128,2048]{1,0:T(8,128)(2,1)} fusion(f32[128,2048]{1,0:T(8,128)} %get-tuple-element.12, bf16[256,2048]{1,0:T(8,128)(2,1)} %bitcast.71, f32[128]{0:T(128)S(1)} %bitcast.79, s32[128]{0:T(128)S(1)} %copy-done.6), kind=kOutput, calls=%fused_computation.15 | convolution fusion | flops 135036928 | bytes 2622464 | tf_op jit(solution)/shard_map/dot_general | solution.py:434
  (29 shorter events, 2.6 us)
Async XLA Ops:
  0.6 122.1 %copy-start = (bf16[1,704,2048]{2,1,0:T(8,128)(2,1)S(1)}, bf16[1,704,2048]{2,1,0:T(8,128)(2,1)}, u32[]{:S(2)}) copy-start(bf16[1,704,2048]{2,1,0:T(8,128)(2,1)} %param.25) | copy-start | bytes 8650756
  54.1 3.9 %copy-start.1 = (bf16[128,128]{1,0:T(8,128)(2,1)S(1)}, bf16[128,128]{1,0:T(8,128)(2,1)}, u32[]{:S(2)}) copy-start(bf16[128,128]{1,0:T(8,128)(2,1)} %param.16) | copy-start | bytes 98308
  54.1 3.9 %copy-start.4 = (f32[2048]{0:T(1024)S(1)}, f32[2048]{0:T(1024)}, u32[]{:S(2)}) copy-start(f32[2048]{0:T(1024)} %mul.96) | copy-start | bytes 24580
  58.0 7.0 %copy-start.2 = (bf16[2048,16]{0,1:T(8,128)(2,1)S(1)}, bf16[2048,16]{0,1:T(8,128)(2,1)}, u32[]{:S(2)}) copy-start(bf16[2048,16]{0,1:T(8,128)(2,1)} %param.21) | copy-start | bytes 196612
  58.0 7.0 %copy-start.3 = (f32[2048]{0:T(1024)S(1)}, f32[2048]{0:T(1024)}, u32[]{:S(2)}) copy-start(f32[2048]{0:T(1024)} %param.20) | copy-start | bytes 24580
  58.1 9.2 %copy-start.6 = (s32[128]{0:T(128)S(1)}, s32[128]{0:T(128)}, u32[]{:S(2)}) copy-start(s32[128]{0:T(128)} %fusion.36) | copy-start | bytes 1540
  130.4 35.0 %copy-start.5 = (f32[1,128]{1,0:T(1,128)S(1)}, f32[1,128]{1,0:T(1,128)}, u32[]{:S(2)}) copy-start(f32[1,128]{1,0:T(1,128)} %balance.1) | copy-start | bytes 1540

commit v2 on v1

--- a/solution.py
+++ b/solution.py
@@ -144,172 +144,199 @@
     )(sent)
 
 
-def dispatch_kernel(devices, packed_ref, kernel_ref, rows_ref, table_ref,
-                    go_send, go_recv, pass_send, pass_recv, table_send, table_recv, own_sem):
-    me = own_index()
+def expert_kernel(devices, group, packed_ref, kernel_ref, gate_hbm, up_hbm, down_hbm, out_ref, table_ref,
+                  rows, halves, partial, summed, gate, up, down, block,
+                  go_send, go_recv, pass_send, pass_recv, swap_send, swap_recv, back_send, back_recv,
+                  near_send, near_recv, far_send, far_recv, own_sem, weight_sem):
+    line, spot = lax.axis_index("seq"), lax.axis_index("exp")
+    lines, spots = lax.axis_size("seq"), lax.axis_size("exp")
+    me = line * spots + spot
     side, mine = me % 2, me // 2
     experts = devices // 2
     partner = me + 1 - 2 * side
-
-    def table_copy(peer, slot):
+    capacity, width = packed_ref.shape[1:]
+    turns = experts // group
+
+    def remote(src, dst, send, recv, device):
         return pltpu.make_async_remote_copy(
-            src_ref=kernel_ref, dst_ref=table_ref.at[slot], send_sem=table_send.at[peer],
-            recv_sem=table_recv.at[slot], device_id=place(peer), device_id_type=MESH)
+            src_ref=src, dst_ref=dst, send_sem=send, recv_sem=recv, device_id=device, device_id_type=MESH)
 
     def row_copy(other, slot):
-        return pltpu.make_async_remote_copy(
-            src_ref=packed_ref.at[other], dst_ref=rows_ref.at[side, slot], send_sem=go_send.at[other],
-            recv_sem=go_recv.at[slot], device_id=place(2 * other + side), device_id_type=MESH)
+        return remote(packed_ref.at[other], rows.at[side, slot], go_send.at[other], go_recv.at[slot],
+                      place(2 * other + side))
 
     def pass_copy(at, slot):
-        return pltpu.make_async_remote_copy(
-            src_ref=rows_ref.at[side, slot], dst_ref=rows_ref.at[at, slot], send_sem=pass_send.at[slot],
-            recv_sem=pass_recv.at[slot], device_id=place(partner), device_id_type=MESH)
-
-    own_rows = pltpu.make_async_copy(packed_ref.at[mine], rows_ref.at[side, mine], own_sem.at[0])
-    own_table = pltpu.make_async_copy(kernel_ref, table_ref.at[me], own_sem.at[1])
+        return remote(rows.at[side, slot], rows.at[at, slot], pass_send.at[slot], pass_recv.at[slot],
+                      place(partner))
+
+    def swap_copy(slot):
+        return remote(halves.at[1 - side, slot], partial.at[slot], swap_send.at[slot], swap_recv.at[slot],
+                      place(partner))
+
+    def back_copy(other, slot):
+        return remote(summed.at[other], out_ref.at[slot], back_send.at[other], back_recv.at[slot],
+                      place(2 * other + side))
+
+    def near_copy(other, slot):
+        return remote(kernel_ref, table_ref.at[line, slot], near_send.at[other], near_recv.at[slot],
+                      (line, other))
+
+    def far_copy(other, slot):
+        return remote(table_ref.at[line], table_ref.at[slot], far_send.at[other], far_recv.at[slot],
+                      (other, spot))
+
+    own_rows = pltpu.make_async_copy(packed_ref.at[mine], rows.at[side, mine], own_sem.at[0])
+    own_table = pltpu.make_async_copy(kernel_ref, table_ref.at[line, spot], own_sem.at[1])
     own_rows.start()
     own_table.start()
+    loads = [
+        pltpu.make_async_copy(gate_hbm, gate, weight_sem.at[0]),
+        pltpu.make_async_copy(up_hbm, up, weight_sem.at[1]),
+        pltpu.make_async_copy(down_hbm, down, weight_sem.at[2]),
+    ]
+    for load in loads:
+        load.start()
     meet_all(me, devices)
 
-    @pl.loop(1, devices)
-    def _(step):
-        table_copy((me + step) % devices, me).start()
-
     @pl.loop(1, experts)
     def _(step):
         row_copy((mine + step) % experts, mine).start()
+
+    @pl.loop(1, spots)
+    def _(step):
+        near_copy((spot + step) % spots, spot).start()
 
     own_rows.wait()
     pass_copy(side, mine).start()
-
-    @pl.loop(1, experts)
-    def _(step):
-        source = (mine + experts - step) % experts
-        row_copy(source, source).wait_recv()
-        pass_copy(side, source).start()
-
-    own_table.wait()
-
-    @pl.loop(1, devices)
-    def _(step):
-        peer = (me + devices - step) % devices
-        table_copy(peer, peer).wait_recv()
-        table_copy(peer, peer).wait_send()
+    for load in loads:
+        load.wait()
+
+    def source_of(turn, at):
+        return (mine + 2 * experts - (turn * group + at)) % experts
+
+    @pl.loop(0, turns + 2)
+    def _(turn):
+        @pl.when(turn < turns)
+        def _():
+            @pl.loop(0, group)
+            def _(at):
+                @pl.when(turn * group + at > 0)
+                def _():
+                    source = source_of(turn, at)
+                    row_copy(source, source).wait_recv()
+                    pass_copy(side, source).start()
+
+        @pl.when((turn >= 1) & (turn <= turns))
+        def _():
+            @pl.loop(0, group)
+            def _(at):
+                pass_copy(1 - side, source_of(turn - 1, at)).wait_recv()
+
+            sources = [source_of(turn - 1, at) for at in range(group)]
+            places = [(k, source, (k * group + at) * capacity)
+                      for k in range(2) for at, source in enumerate(sources)]
+            for k, source, start in places:
+                block[start:start + capacity] = rows[k, source]
+            taken = block[...]
+            across = (((1,), (1,)), ((), ()))
+            gate_val = lax.dot_general(taken, gate[...], across, preferred_element_type=jnp.float32)
+            up_val = lax.dot_general(taken, up[...], across, preferred_element_type=jnp.float32)
+            hidden = (gate_val / (1.0 + jnp.exp(-gate_val)) * up_val).astype(jnp.bfloat16)
+            piece = 512
+            for column in range(0, width, piece):
+                made = jnp.dot(hidden, down[:, column:column + piece], preferred_element_type=jnp.float32)
+                made = made.astype(halves.dtype)
+                for k, source, start in places:
+                    halves[k, source, :, column:column + piece] = made[start:start + capacity]
+
+            @pl.loop(0, group)
+            def _(at):
+                swap_copy(source_of(turn - 1, at)).start()
+
+        @pl.when(turn >= 2)
+        def _():
+            @pl.loop(0, group)
+            def _(at):
+                source = source_of(turn - 2, at)
+                swap_copy(source).wait_recv()
+                summed[source] = (
+                    halves[side, source].astype(jnp.float32) + partial[source].astype(jnp.float32)
+                ).astype(summed.dtype)
+
+                @pl.when((turn - 2) * group + at > 0)
+                def _():
+                    back_copy(source, mine).start()
+
+        @pl.when(turn == 1)
+        def _():
+            own_table.wait()
+
+            @pl.loop(1, spots)
+            def _(step):
+                near_copy((spot + step) % spots, (spot + step) % spots).wait_recv()
+
+            @pl.loop(1, lines)
+            def _(step):
+                far_copy((line + step) % lines, line).start()
+
+    own_out = pltpu.make_async_copy(summed.at[mine], out_ref.at[mine], own_sem.at[0])
+    own_out.start()
+
+    @pl.loop(1, lines)
+    def _(step):
+        other = (line + step) % lines
+        far_copy(other, other).wait_recv()
+        far_copy(other, other).wait_send()
+
+    @pl.loop(1, spots)
+    def _(step):
+        near_copy((spot + step) % spots, spot).wait_send()
 
     @pl.loop(0, experts)
     def _(step):
-        source = (mine + experts - step) % experts
-        pass_copy(1 - side, source).wait_recv()
-        pass_copy(side, source).wait_send()
+        pass_copy(side, step).wait_send()
+        swap_copy(step).wait_send()
 
     @pl.loop(1, experts)
     def _(step):
         other = (mine + step) % experts
         row_copy(other, other).wait_send()
-
-
-def dispatch(packed, kernel):
+        back_copy(other, other).wait_recv()
+        back_copy(other, other).wait_send()
+
+    own_out.wait()
+
+
+def expert_layer(packed, kernel, gate_half, up_half, down_half):
     devices = device_count()
+    lines, spots = lax.axis_size("seq"), lax.axis_size("exp")
     experts, capacity, width = packed.shape
+    hidden_units = down_half.shape[0]
+    group = 4
     dma = pltpu.SemaphoreType.DMA
     vmem = pl.BlockSpec(memory_space=pltpu.VMEM)
+    anywhere = pl.BlockSpec(memory_space=pl.ANY)
+    single = pltpu.VMEM((experts, capacity, width), packed.dtype)
+    double = pltpu.VMEM((2, experts, capacity, width), packed.dtype)
+    weights = pltpu.VMEM((hidden_units, width), packed.dtype)
+    each = dma((experts,))
     return pl.pallas_call(
-        functools.partial(dispatch_kernel, devices),
+        functools.partial(expert_kernel, devices, group),
         out_shape=(
-            jax.ShapeDtypeStruct((2, experts, capacity, width), packed.dtype),
-            jax.ShapeDtypeStruct((devices, *kernel.shape), kernel.dtype),
+            jax.ShapeDtypeStruct((experts, capacity, width), packed.dtype),
+            jax.ShapeDtypeStruct((lines, spots, *kernel.shape), kernel.dtype),
         ),
-        in_specs=[vmem, vmem],
+        in_specs=[vmem, vmem, anywhere, anywhere, anywhere],
         out_specs=(vmem, vmem),
         scratch_shapes=[
-            dma((experts,)), dma((experts,)), dma((experts,)), dma((experts,)),
-            dma((devices,)), dma((devices,)), dma((2,)),
+            double, double, single, single, weights, weights, weights,
+            pltpu.VMEM((2 * group * capacity, width), packed.dtype),
+            each, each, each, each, each, each, each, each,
+            dma((spots,)), dma((spots,)), dma((lines,)), dma((lines,)), dma((2,)), dma((3,)),
         ],
         compiler_params=pltpu.CompilerParams(collective_id=1, has_side_effects=True),
-        name="dispatch_rows",
-    )(packed, kernel)
-
-
-def collect_kernel(devices, half_ref, out_ref, partial, summed,
-                   swap_send, swap_recv, back_send, back_recv, own_sem):
-    me = own_index()
-    side, mine = me % 2, me // 2
-    experts = devices // 2
-    partner = me + 1 - 2 * side
-
-    def swap_copy(slot):
-        return pltpu.make_async_remote_copy(
-            src_ref=half_ref.at[1 - side, slot], dst_ref=partial.at[slot], send_sem=swap_send.at[slot],
-            recv_sem=swap_recv.at[slot], device_id=place(partner), device_id_type=MESH)
-
-    def back_copy(other, slot):
-        return pltpu.make_async_remote_copy(
-            src_ref=summed.at[other], dst_ref=out_ref.at[slot], send_sem=back_send.at[other],
-            recv_sem=back_recv.at[slot], device_id=place(2 * other + side), device_id_type=MESH)
-
-    def add_up(slot):
-        swap_copy(slot).wait_recv()
-        summed[slot] = (
-            half_ref[side, slot].astype(jnp.float32) + partial[slot].astype(jnp.float32)
-        ).astype(summed.dtype)
-
-    barrier = pltpu.get_barrier_semaphore()
-
-    @pl.loop(1, experts)
-    def _(step):
-        pl.semaphore_signal(
-            barrier, inc=1, device_id=place(2 * ((mine + step) % experts) + side), device_id_type=MESH
-        )
-
-    pl.semaphore_signal(barrier, inc=1, device_id=place(partner), device_id_type=MESH)
-    pl.semaphore_wait(barrier, experts)
-
-    @pl.loop(1, experts + 1)
-    def _(step):
-        swap_copy((mine + step) % experts).start()
-
-    @pl.loop(1, experts)
-    def _(step):
-        other = (mine + step) % experts
-        add_up(other)
-        back_copy(other, mine).start()
-
-    add_up(mine)
-    own = pltpu.make_async_copy(summed.at[mine], out_ref.at[mine], own_sem)
-    own.start()
-
-    @pl.loop(1, experts)
-    def _(step):
-        other = (mine + experts - step) % experts
-        back_copy(other, other).wait_recv()
-        back_copy(other, other).wait_send()
-
-    @pl.loop(0, experts)
-    def _(step):
-        swap_copy(step).wait_send()
-
-    own.wait()
-
-
-def collect(halves):
-    devices = device_count()
-    _, experts, capacity, width = halves.shape
-    dma = pltpu.SemaphoreType.DMA
-    vmem = pl.BlockSpec(memory_space=pltpu.VMEM)
-    block = pltpu.VMEM((experts, capacity, width), halves.dtype)
-    return pl.pallas_call(
-        functools.partial(collect_kernel, devices),
-        out_shape=jax.ShapeDtypeStruct((experts, capacity, width), halves.dtype),
-        in_specs=[vmem],
-        out_specs=vmem,
-        scratch_shapes=[
-            block, block,
-            dma((experts,)), dma((experts,)), dma((experts,)), dma((experts,)), dma,
-        ],
-        compiler_params=pltpu.CompilerParams(collective_id=2, has_side_effects=True),
-        name="collect_rows",
-    )(halves)
+        name="expert_layer",
+    )(packed, kernel, gate_half.T, up_half.T, down_half)
 
 
 def balance_kernel(table_ref, own_ref, hot_ref, weight_ref):
@@ -365,13 +392,6 @@
     decay_mix = decay_mix.astype(jnp.bfloat16)
     inner_part = jnp.einsum("hts,shp->thp", decay_mix, values, preferred_element_type=jnp.float32)
     return (inner_part.reshape(length, row_width), cumulative, block_state)
-
-
-def feed_forward(flat, gate_half, up_half, down_half):
-    gate_val = jnp.dot(flat, gate_half, preferred_element_type=jnp.float32)
-    up_val = jnp.dot(flat, up_half, preferred_element_type=jnp.float32)
-    hidden = (jax.nn.silu(gate_val) * up_val).astype(jnp.bfloat16)
-    return jnp.dot(hidden, down_half, preferred_element_type=jnp.float32).astype(jnp.bfloat16)
 
 
 def per_device(
@@ -410,7 +430,7 @@
     normed = (mixed * scale * norm_gain[None, :]).astype(jnp.bfloat16)
     kernel = jnp.exp(jnp.einsum("de,td->et", router, normed, preferred_element_type=jnp.float32))
     experts = router.shape[1]
-    capacity = 2 * length // experts
+    capacity = max(16, 2 * length // experts)
     chosen = assignment[:, 0]
     hot = (chosen[:, None] == jnp.arange(experts, dtype=jnp.int32)[None, :]).astype(jnp.float32)
     upto = (jnp.arange(length)[:, None] >= jnp.arange(length)[None, :]).astype(jnp.bfloat16)
@@ -422,15 +442,8 @@
     ).astype(jnp.bfloat16)
     packed = jnp.einsum("ts,td->sd", spread, normed, preferred_element_type=jnp.float32)
     packed = packed.astype(jnp.bfloat16).reshape(experts, capacity, model_width)
-    arrived, table = dispatch(packed, kernel)
-    route_weight = balance(table, kernel, hot.T)[0]
-    halves = feed_forward(
-        arrived.reshape(2 * experts * capacity, model_width),
-        expert_gate[0],
-        expert_up[0],
-        expert_down[0],
-    )
-    summed = collect(halves.reshape(2, experts, capacity, model_width))
+    summed, table = expert_layer(packed, kernel, expert_gate[0], expert_up[0], expert_down[0])
+    route_weight = balance(table.reshape(-1, experts, length), kernel, hot.T)[0]
     expert_out = jnp.dot(
         spread, summed.reshape(experts * capacity, model_width), preferred_element_type=jnp.float32
     )

time: 170 us -> 129 us (0.76); the launches traced: 168 us -> 129 us
  matrix products: 33.9 us -> 13 us
  Pallas kernels: 121 us -> 110 us
  local copies, waits for them, and re-layouts: 6.99 us -> 2.93 us
  other arithmetic: 5.11 us -> 1.98 us
    dot_general x2 -> x0, matrix products: 12.9 us -> none  [the longest x1 7.62 us: feed_forward(): jnp.dot(hidden, down_half, preferred_element_type=jnp.float32)]
    pallas_call x2 -> x1, Pallas kernels: 79.5 us -> 68.2 us  [expert_layer(): pl.pallas_call(functools.partial(expert_kernel, devices, group), out_shap...]
where the time goes in v2:
time: 129 us
  Pallas kernels  110 us (85%)
  matrix products  13 us (10%)
  local copies, waits for them, and re-layouts  2.93 us (2%)
  other arithmetic  1.98 us (2%)
    pallas_call x1, Pallas kernels, expert_layer(): pl.pallas_call(functools.partial(expert_kernel, devices, group), out_shap...  68.2 us
    pallas_call x1, Pallas kernels, entering(): pl.pallas_call(functools.partial(entry_kernel, devices), out_shape=jax.Sh...  38.8 us
    dot_general x1, matrix products, per_device(): jnp.dot(scan_out, out_proj, preferred_element_type=jnp.float32)  5.6 us
    pallas_call x1, Pallas kernels, balance(): pl.pallas_call(balance_kernel, out_shape=jax.ShapeDtypeStruct((1, own.sha...  2.97 us

profile of v2, /device:TPU:1, one launch (start us, length us, event | category | flops | bytes accessed | tf_op | source)
XLA Modules:
  0.0 128.7 jit_solution(16000708382880243280)
XLA Ops:
  0.7 0.8 copy.22
  1.5 0.2 reduce_window_sum.11
  1.8 1.3 %copy.27 = bf16[128,2048]{0,1:T(8,128)(2,1)S(1)} copy(bf16[128,2048]{1,0:T(8,128)(2,1)} %param.14) | data formatting | bytes 1048576 | tf_op args[1]
  3.1 0.1 fusion.9
  3.3 0.3 convolution_convert_fusion.1
  3.6 0.1 broadcast_in_dim.21
  3.7 0.1 reshape.94
  3.8 0.1 pad.4.clone
  3.9 0.1 maximum_maximum_fusion
  4.0 0.9 pad_maximum_fusion.src_ref
  4.9 38.8 %entry_states.1 = bf16[128,2048]{1,0:T(8,128)(2,1)} custom-call(bf16[2,80,2048]{2,1,0:T(8,128)(2,1)} %pad_maximum_fusion.src_ref), custom_call_target="tpu_custom_call" | custom-call | tf_op jit(solution)/shard_map/entry_states/pallas_call | solution.py:132
  43.8 0.1 copy.23
  43.8 0.1 fusion.25
  44.1 1.9 %fusion.8 = f32[32,128,64]{1,2,0:T(8,128)} fusion(bf16[128,32,64]{0,2,1:T(8,128)(2,1)S(1)} %bitcast.59, f32[128,128]{1,0:T(8,128)S(1)} %fusion.25, f32[32,128]{1,0:T(8,128)S(1)} %copy.26, f32[32,128]{1,0:T(8,128)S(1)} %copy.23, pred[128,128]{1,0:T(8,128)(4,1)S(1)} %iota_compare_fusion.3), kind=kOutput, calls=%fused_computation.18 | convolution fusion | flops 70254592 | bytes 1687552 | tf_op jit(solution)/shard_map/hts,shp->thp/dot_general | solution.py:393
  46.0 0.1 broadcast_in_dim.19
  46.2 0.1 mul.89
  46.3 5.6 %multiply_reduce_fusion = (f32[128]{0:T(128)S(1)}, f32[128,2048]{1,0:T(8,128)S(1)}) fusion(bf16[2048,2048]{1,0:T(8,128)(2,1)} %param.19, f32[128,2048]{0,1:T(8,128)} %bitcast.66, f32[128,2048]{0,1:T(8,128)S(1)} %bitcast.60, bf16[128,2048]{1,0:T(8,128)(2,1)S(1)} %copy-done.1, bf16[128,128]{1,0:T(8,128)(2,1)S(1)} %copy-done.2, ...), kind=kOutput, calls=%fused_computation.21 | convolution fusion | flops 1143472000 | bytes 13148672 | tf_op jit(solution)/shard_map/dot_general | solution.py:426
  51.9 0.9 fusion.6.kernel_ref.own_ref
  52.9 0.2 fusion.7
  53.0 1.6 %convolution_convert_fusion = bf16[256,2048]{1,0:T(8,128)(2,1)} fusion(s32[128]{0:T(128)S(1)} %fusion.22, f32[128,2048]{1,0:T(8,128)S(1)} %get-tuple-element.12, f32[2048]{0:T(1024)S(1)} %copy-done.4, f32[128]{0:T(128)S(1)} %add_rsqrt_fusion), kind=kOutput, calls=%fused_computation | convolution fusion | flops 135561216 | bytes 2106368 | tf_op jit(solution)/shard_map/ts,td->sd/dot_general | solution.py:443
  54.6 68.2 %expert_layer.1 = (bf16[16,16,2048]{2,1,0:T(8,128)(2,1)}, f32[4,8,16,128]{3,2,1,0:T(8,128)}) custom-call(bf16[16,16,2048]{2,1,0:T(8,128)(2,1)} %bitcast.61, f32[16,128]{1,0:T(8,128)} %fusion.6.kernel_ref.own_ref, bf16[704,2048]{1,0:T(8,128)(2,1)} %bitcast.62, bf16[704,2048]{1,0:T(8,128)(2,1)} %bitcast.63, bf16[704,2048]{1,0:T(8,128)(2,1)} %bitcast.64), custom_call_target="tpu_custom_call" | custom-call | tf_op jit(solution)/shard_map/expert_layer/pallas_call | solution.py:323
  122.8 0.6 fusion.20.hot_ref
  123.4 3.0 %balance.1 = f32[1,128]{1,0:T(1,128)} custom-call(f32[32,16,128]{2,1,0:T(8,128)} %bitcast.69, f32[16,128]{1,0:T(8,128)} %fusion.6.kernel_ref.own_ref, f32[16,128]{1,0:T(8,128)} %fusion.20.hot_ref), custom_call_target="tpu_custom_call" | custom-call | tf_op jit(solution)/shard_map/balance/pallas_call | solution.py:363
  126.4 2.4 %fusion.5 = bf16[128,2048]{1,0:T(8,128)(2,1)} fusion(f32[128,2048]{1,0:T(8,128)S(1)} %get-tuple-element.12, bf16[256,2048]{1,0:T(8,128)(2,1)} %bitcast.67, f32[128]{0:T(128)} %bitcast.70, s32[128]{0:T(128)S(1)} %fusion.22), kind=kOutput, calls=%fused_computation.9 | convolution fusion | flops 135036928 | bytes 2622464 | tf_op jit(solution)/shard_map/dot_general | solution.py:447
  (26 shorter events, 0.4 us)
Async XLA Ops:
  0.6 51.3 %copy-start = (bf16[2048,16]{0,1:T(8,128)(2,1)S(1)}, bf16[2048,16]{0,1:T(8,128)(2,1)}, u32[]{:S(2)}) copy-start(bf16[2048,16]{0,1:T(8,128)(2,1)} %param.21) | copy-start | bytes 196612
  0.6 2.6 %copy-start.3 = (bf16[128,128]{1,0:T(8,128)(2,1)S(1)}, bf16[128,128]{1,0:T(8,128)(2,1)}, u32[]{:S(2)}) copy-start(bf16[128,128]{1,0:T(8,128)(2,1)} %param.15) | copy-start | bytes 98308
  3.3 40.6 %copy-start.2 = (bf16[128,128]{1,0:T(8,128)(2,1)S(1)}, bf16[128,128]{1,0:T(8,128)(2,1)}, u32[]{:S(2)}) copy-start(bf16[128,128]{1,0:T(8,128)(2,1)} %param.16) | copy-start | bytes 98308
  44.0 2.1 %copy-start.5 = (f32[32]{0:T(128)S(1)}, f32[32]{0:T(128)}, u32[]{:S(2)}) copy-start(f32[32]{0:T(128)} %param.18) | copy-start | bytes 388
  44.0 2.2 %copy-start.1 = (bf16[128,2048]{1,0:T(8,128)(2,1)S(1)}, bf16[128,2048]{1,0:T(8,128)(2,1)}, u32[]{:S(2)}) copy-start(bf16[128,2048]{1,0:T(8,128)(2,1)} %entry_states.1) | copy-start | bytes 1572868
  46.3 5.6 %copy-start.4 = (f32[2048]{0:T(1024)S(1)}, f32[2048]{0:T(1024)}, u32[]{:S(2)}) copy-start(f32[2048]{0:T(1024)} %param.20) | copy-start | bytes 24580
  46.3 6.6 %copy-start.6 = (s32[128,1]{0,1:T(1,128)S(1)}, s32[128,1]{0,1:T(1,128)}, u32[]{:S(2)}) copy-start(s32[128,1]{0,1:T(1,128)} %param.22) | copy-start | bytes 1540

commit v3 on v2

--- a/solution.py
+++ b/solution.py
@@ -9,7 +9,6 @@
 
 SINK_ITERS = 8
 LANES = 128
-TOTAL_ROWS = 16
 MESH = pl.DeviceIdType.MESH
 
 
@@ -38,114 +37,122 @@
     pl.semaphore_wait(barrier, devices - 1)
 
 
-def entry_kernel(devices, src_ref, out_ref, arrived, entries, go_send, go_recv, back_send, back_recv, own_sem):
+def entry_kernel(devices, pieces, src_ref, factor_ref, out_ref, arrived, entries, factors,
+                 go_send, go_recv, factor_send, factor_recv, back_send, back_recv, own_sem):
     me = own_index()
     groups = out_ref.shape[1] // LANES
-    rows = entries.shape[1]
-
-    def part_of(flat):
-        return src_ref.at[flat // groups, :, pl.ds(pl.multiple_of((flat % groups) * LANES, LANES), LANES)]
-
-    def region_of(flat):
-        return out_ref.at[
-            pl.ds(pl.multiple_of((flat // groups) * rows, rows), rows),
+    rows = arrived.shape[2]
+
+    def region(ref, flat, piece):
+        return ref.at[
+            pl.ds(pl.multiple_of(((flat // groups) * pieces + piece) * rows, rows), rows),
             pl.ds(pl.multiple_of((flat % groups) * LANES, LANES), LANES),
         ]
 
-    def outgoing(peer):
+    def remote(src, dst, send, recv, peer):
         return pltpu.make_async_remote_copy(
-            src_ref=part_of(peer), dst_ref=arrived.at[me], send_sem=go_send.at[peer],
-            recv_sem=go_recv.at[me], device_id=place(peer), device_id_type=MESH)
-
-    def incoming(peer):
-        return pltpu.make_async_remote_copy(
-            src_ref=part_of(peer), dst_ref=arrived.at[peer], send_sem=go_send.at[peer],
-            recv_sem=go_recv.at[peer], device_id=place(peer), device_id_type=MESH)
-
-    def returning(peer):
-        return pltpu.make_async_remote_copy(
-            src_ref=entries.at[peer], dst_ref=region_of(me), send_sem=back_send.at[peer],
-            recv_sem=back_recv.at[me], device_id=place(peer), device_id_type=MESH)
-
-    def returned(peer):
-        return pltpu.make_async_remote_copy(
-            src_ref=entries.at[peer], dst_ref=region_of(peer), send_sem=back_send.at[peer],
-            recv_sem=back_recv.at[peer], device_id=place(peer), device_id_type=MESH)
-
-    own = pltpu.make_async_copy(part_of(me), arrived.at[me], own_sem)
-    own.start()
+            src_ref=src, dst_ref=dst, send_sem=send, recv_sem=recv, device_id=place(peer), device_id_type=MESH)
+
+    def state_copy(piece, peer, slot):
+        return remote(region(src_ref, peer, piece), arrived.at[piece, slot], go_send.at[piece, peer],
+                      go_recv.at[piece, slot], peer)
+
+    def factor_copy(peer, slot):
+        return remote(factor_ref.at[peer % groups], factors.at[slot], factor_send.at[peer],
+                      factor_recv.at[slot], peer)
+
+    def entry_copy(piece, peer, slot):
+        return remote(entries.at[piece, peer], region(out_ref, slot, piece), back_send.at[piece, peer],
+                      back_recv.at[piece, slot], peer)
+
+    own_factor = pltpu.make_async_copy(factor_ref.at[me % groups], factors.at[me], own_sem.at[0])
+    own_state = [
+        pltpu.make_async_copy(region(src_ref, me, piece), arrived.at[piece, me], own_sem.at[1 + piece])
+        for piece in range(pieces)
+    ]
+    own_factor.start()
+    for piece in range(pieces):
+        own_state[piece].start()
     meet_all(me, devices)
 
     @pl.loop(1, devices)
     def _(step):
-        outgoing((me + step) % devices).start()
-
-    own.wait()
+        peer = (me + step) % devices
+        factor_copy(peer, me).start()
+        state_copy(0, peer, me).start()
+
+    for piece in range(1, pieces):
+        @pl.loop(1, devices)
+        def _(step):
+            state_copy(piece, (me + step) % devices, me).start()
+
+    own_factor.wait()
+    for piece in range(pieces):
+        own_state[piece].wait()
+
+        @pl.loop(1, devices)
+        def _(step):
+            peer = (me + devices - step) % devices
+            if piece == 0:
+                factor_copy(peer, peer).wait_recv()
+            state_copy(piece, peer, peer).wait_recv()
+
+        def advance(k, state):
+            entries[piece, k] = state.astype(entries.dtype)
+            return factors[k] * state + arrived[piece, k].astype(jnp.float32)
+
+        lax.fori_loop(0, devices, advance, jnp.zeros((rows, LANES), jnp.float32))
+
+        @pl.loop(1, devices)
+        def _(step):
+            entry_copy(piece, (me + step) % devices, me).start()
+
+    own_back = [
+        pltpu.make_async_copy(entries.at[piece, me], region(out_ref, me, piece), own_sem.at[1 + piece])
+        for piece in range(pieces)
+    ]
+    for piece in range(pieces):
+        own_back[piece].start()
 
     @pl.loop(1, devices)
     def _(step):
-        incoming((me + devices - step) % devices).wait_recv()
-
-    def advance(k, state):
-        entries[k] = state.astype(entries.dtype)
-        block = arrived[k]
-        total = jnp.sum(block[rows:rows + TOTAL_ROWS].astype(jnp.float32), axis=0, keepdims=True)
-        return jnp.exp(total) * state + block[:rows].astype(jnp.float32)
-
-    lax.fori_loop(0, devices, advance, jnp.zeros((rows, LANES), jnp.float32))
-
-    @pl.loop(1, devices)
-    def _(step):
-        returning((me + step) % devices).start()
-
-    own_back = pltpu.make_async_copy(entries.at[me], region_of(me), own_sem)
-    own_back.start()
-
-    @pl.loop(1, devices)
-    def _(step):
         peer = (me + devices - step) % devices
-        returned(peer).wait_recv()
-        outgoing(peer).wait_send()
-        returning(peer).wait_send()
-
-    own_back.wait()
-
-
-def entering(block_state, total):
+        factor_copy(peer, peer).wait_send()
+        for piece in range(pieces):
+            state_copy(piece, peer, peer).wait_send()
+            entry_copy(piece, peer, peer).wait_recv()
+            entry_copy(piece, peer, peer).wait_send()
+
+    for piece in range(pieces):
+        own_back[piece].wait()
+
+
+def entering(block_state, factor):
     devices = device_count()
     state_size, width = block_state.shape
-    parts = devices // (width // LANES)
-    rows = state_size // parts
-    high = total.astype(jnp.bfloat16)
-    low = (total - high.astype(jnp.float32)).astype(jnp.bfloat16)
-    totals = jnp.concatenate(
-        [high[None], low[None], jnp.zeros((TOTAL_ROWS - 2, width), jnp.bfloat16)], axis=0
-    )
-    sent = jnp.concatenate(
-        [
-            block_state.astype(jnp.bfloat16).reshape(parts, rows, width),
-            jnp.broadcast_to(totals[None], (parts, TOTAL_ROWS, width)),
-        ],
-        axis=1,
-    )
+    groups = width // LANES
+    rows = state_size * groups // devices
+    pieces = 2 if rows % 32 == 0 else 1
     dma = pltpu.SemaphoreType.DMA
+    vmem = pl.BlockSpec(memory_space=pltpu.VMEM)
+    held = pltpu.VMEM((pieces, devices, rows // pieces, LANES), jnp.bfloat16)
+    each = dma((pieces, devices))
     return pl.pallas_call(
-        functools.partial(entry_kernel, devices),
+        functools.partial(entry_kernel, devices, pieces),
         out_shape=jax.ShapeDtypeStruct((state_size, width), jnp.bfloat16),
-        in_specs=[pl.BlockSpec(memory_space=pltpu.VMEM)],
-        out_specs=pl.BlockSpec(memory_space=pltpu.VMEM),
+        in_specs=[vmem, vmem],
+        out_specs=vmem,
         scratch_shapes=[
-            pltpu.VMEM((devices, rows + TOTAL_ROWS, LANES), jnp.bfloat16),
-            pltpu.VMEM((devices, rows, LANES), jnp.bfloat16),
-            dma((devices,)), dma((devices,)), dma((devices,)), dma((devices,)), dma,
+            held, held, pltpu.VMEM((devices, 1, LANES), jnp.float32),
+            each, each, dma((devices,)), dma((devices,)), each, each, dma((1 + pieces,)),
         ],
         compiler_params=pltpu.CompilerParams(collective_id=0, has_side_effects=True),
         name="entry_states",
-    )(sent)
-
-
-def expert_kernel(devices, group, packed_ref, kernel_ref, gate_hbm, up_hbm, down_hbm, out_ref, table_ref,
-                  rows, halves, partial, summed, gate, up, down, block,
+    )(block_state.astype(jnp.bfloat16), factor.reshape(groups, 1, LANES))
+
+
+def expert_kernel(devices, group, packed_ref, kernel_ref, hot_ref, gate_hbm, up_hbm, down_hbm, out_ref, weight_ref,
+                  table_ref, rows, halves, partial, summed, gate, up, down, block,
                   go_send, go_recv, pass_send, pass_recv, swap_send, swap_recv, back_send, back_recv,
                   near_send, near_recv, far_send, far_recv, own_sem, weight_sem):
     line, spot = lax.axis_index("seq"), lax.axis_index("exp")
@@ -288,6 +295,22 @@
         far_copy(other, other).wait_recv()
         far_copy(other, other).wait_send()
 
+    choices, length = kernel_ref.shape
+
+    def sweep(_, column):
+        def add(at, totals):
+            part = table_ref[at]
+            row_scale = 1.0 / jnp.sum(part * column[None], axis=1, keepdims=True)
+            return totals + jnp.sum(part * row_scale, axis=0)
+
+        totals = lax.fori_loop(0, lines, add, jnp.zeros((choices, length), jnp.float32))
+        return 1.0 / jnp.sum(totals, axis=1, keepdims=True)
+
+    column = lax.fori_loop(0, SINK_ITERS, sweep, jnp.ones((choices, 1), jnp.float32))
+    weighted = kernel_ref[...] * column
+    picked = jnp.sum(jnp.where(hot_ref[...] > 0.0, weighted, 0.0), axis=0, keepdims=True)
+    weight_ref[...] = choices * picked / jnp.sum(weighted, axis=0, keepdims=True)
+
     @pl.loop(1, spots)
     def _(step):
         near_copy((spot + step) % spots, spot).wait_send()
@@ -307,7 +330,7 @@
     own_out.wait()
 
 
-def expert_layer(packed, kernel, gate_half, up_half, down_half):
+def expert_layer(packed, kernel, hot, gate_half, up_half, down_half):
     devices = device_count()
     lines, spots = lax.axis_size("seq"), lax.axis_size("exp")
     experts, capacity, width = packed.shape
@@ -324,11 +347,12 @@
         functools.partial(expert_kernel, devices, group),
         out_shape=(
             jax.ShapeDtypeStruct((experts, capacity, width), packed.dtype),
-            jax.ShapeDtypeStruct((lines, spots, *kernel.shape), kernel.dtype),
+            jax.ShapeDtypeStruct((1, kernel.shape[1]), kernel.dtype),
         ),
-        in_specs=[vmem, vmem, anywhere, anywhere, anywhere],
+        in_specs=[vmem, vmem, vmem, anywhere, anywhere, anywhere],
         out_specs=(vmem, vmem),
         scratch_shapes=[
+            pltpu.VMEM((lines, spots, *kernel.shape), kernel.dtype),
             double, double, single, single, weights, weights, weights,
             pltpu.VMEM((2 * group * capacity, width), packed.dtype),
             each, each, each, each, each, each, each, each,
@@ -336,37 +360,7 @@
         ],
         compiler_params=pltpu.CompilerParams(collective_id=1, has_side_effects=True),
         name="expert_layer",
-    )(packed, kernel, gate_half.T, up_half.T, down_half)
-
-
-def balance_kernel(table_ref, own_ref, hot_ref, weight_ref):
-    devices, experts, length = table_ref.shape
-    some = 8
-
-    def sweep(_, column):
-        def add(k, totals):
-            block = table_ref[pl.ds(pl.multiple_of(k * some, some), some)]
-            row_scale = 1.0 / jnp.sum(block * column[None], axis=1, keepdims=True)
-            return totals + jnp.sum(block * row_scale, axis=0)
-
-        totals = lax.fori_loop(0, devices // some, add, jnp.zeros((experts, length), jnp.float32))
-        return 1.0 / jnp.sum(totals, axis=1, keepdims=True)
-
-    column = lax.fori_loop(0, SINK_ITERS, sweep, jnp.ones((experts, 1), jnp.float32))
-    weighted = own_ref[...] * column
-    picked = jnp.sum(jnp.where(hot_ref[...] > 0.0, weighted, 0.0), axis=0, keepdims=True)
-    weight_ref[...] = experts * picked / jnp.sum(weighted, axis=0, keepdims=True)
-
-
-def balance(table, own, hot):
-    vmem = pl.BlockSpec(memory_space=pltpu.VMEM)
-    return pl.pallas_call(
-        balance_kernel,
-        out_shape=jax.ShapeDtypeStruct((1, own.shape[1]), jnp.float32),
-        in_specs=[vmem, vmem, vmem],
-        out_specs=vmem,
-        name="balance",
-    )(table, own, hot)
+    )(packed, kernel, hot, gate_half.T, up_half.T, down_half)
 
 
 def widen(per_head, width):
@@ -415,7 +409,7 @@
     model_width = residual_in.shape[1]
     values = ssm_input.reshape(length, head_count, head_size)
     inner_part, cumulative, block_state = block_terms(values, ssm_b, ssm_c, log_decay)
-    entry_rounded = entering(block_state, widen(cumulative[-1], row_width))
+    entry_rounded = entering(block_state, widen(jnp.exp(cumulative[-1]), row_width))
     carried = widen(jnp.exp(cumulative), row_width) * jnp.dot(
         ssm_c, entry_rounded, preferred_element_type=jnp.float32
     )
@@ -442,8 +436,10 @@
     ).astype(jnp.bfloat16)
     packed = jnp.einsum("ts,td->sd", spread, normed, preferred_element_type=jnp.float32)
     packed = packed.astype(jnp.bfloat16).reshape(experts, capacity, model_width)
-    summed, table = expert_layer(packed, kernel, expert_gate[0], expert_up[0], expert_down[0])
-    route_weight = balance(table.reshape(-1, experts, length), kernel, hot.T)[0]
+    summed, weight_row = expert_layer(
+        packed, kernel, hot.T, expert_gate[0], expert_up[0], expert_down[0]
+    )
+    route_weight = weight_row[0]
     expert_out = jnp.dot(
         spread, summed.reshape(experts * capacity, model_width), preferred_element_type=jnp.float32
     )

time: 129 us -> 124 us (0.961)
  Pallas kernels: 110 us -> 104 us
    pallas_call x2 -> x1, Pallas kernels: 41.8 us -> 36.2 us  [entering(): pl.pallas_call(functools.partial(entry_kernel, devices, pieces), out_shap...]
    unnamed x16 -> x19, local copies, waits for them, and re-layouts: 2.22 us -> 2.74 us
where the time goes in v3:
time: 124 us
  Pallas kernels  104 us (84%)
  matrix products  13.8 us (11%)
  local copies, waits for them, and re-layouts  4.08 us (3%)
    pallas_call x1, Pallas kernels, expert_layer(): pl.pallas_call(functools.partial(expert_kernel, devices, group), out_shap...  68.3 us
    pallas_call x1, Pallas kernels, entering(): pl.pallas_call(functools.partial(entry_kernel, devices, pieces), out_shap...  36.2 us
    dot_general x1, matrix products, per_device(): jnp.dot(scan_out, out_proj, preferred_element_type=jnp.float32)  5.6 us
    unnamed x19, local copies, waits for them, and re-layouts  2.74 us

profile of v3, /device:TPU:1, one launch (start us, length us, event | category | flops | bytes accessed | tf_op | source)
XLA Modules:
  0.0 124.1 jit_solution(295835597470111536)
XLA Ops:
  0.7 0.8 copy.22
  1.5 0.2 reduce_window_sum.11
  1.7 0.1 exponential_multiply_fusion
  1.8 1.3 %copy.27 = bf16[128,2048]{0,1:T(8,128)(2,1)S(1)} copy(bf16[128,2048]{1,0:T(8,128)(2,1)} %param.14) | data formatting | bytes 1048576 | tf_op args[1]
  3.2 0.1 fusion.10
  3.3 1.1 fusion.6.src_ref
  4.4 0.1 exp.25
  4.5 0.1 broadcast_in_dim.19
  4.6 0.7 broadcast_in_dim.20.factor_ref
  5.3 36.2 %entry_states.1 = bf16[128,2048]{1,0:T(8,128)(2,1)} custom-call(bf16[128,2048]{1,0:T(8,128)(2,1)} %fusion.6.src_ref, f32[16,1,128]{2,1,0:T(1,128)} %broadcast_in_dim.20.factor_ref), custom_call_target="tpu_custom_call" | custom-call | tf_op jit(solution)/shard_map/entry_states/pallas_call | solution.py:140
  41.5 0.1 copy.23
  41.6 0.1 fusion.25
  41.8 1.9 %fusion.9 = f32[32,128,64]{1,2,0:T(8,128)} fusion(bf16[128,32,64]{0,2,1:T(8,128)(2,1)S(1)} %bitcast.57, f32[128,128]{1,0:T(8,128)S(1)} %fusion.25, f32[32,128]{1,0:T(8,128)S(1)} %copy.26, f32[32,128]{1,0:T(8,128)S(1)} %copy.23, pred[128,128]{1,0:T(8,128)(4,1)S(1)} %iota_compare_fusion.3), kind=kOutput, calls=%fused_computation.19 | convolution fusion | flops 70254592 | bytes 1687552 | tf_op jit(solution)/shard_map/hts,shp->thp/dot_general | solution.py:387
  43.8 0.1 broadcast_in_dim.17
  43.9 0.1 broadcast_in_dim.38
  44.0 0.1 mul.89
  44.1 5.6 %multiply_reduce_fusion = (f32[128]{0:T(128)S(1)}, f32[128,2048]{1,0:T(8,128)S(1)}) fusion(bf16[2048,2048]{1,0:T(8,128)(2,1)} %param.19, f32[128,2048]{0,1:T(8,128)} %bitcast.63, f32[128,2048]{0,1:T(8,128)S(1)} %bitcast.58, bf16[128,2048]{1,0:T(8,128)(2,1)S(1)} %copy-done.1, bf16[128,128]{1,0:T(8,128)(2,1)S(1)} %copy-done.2, ...), kind=kOutput, calls=%fused_computation.22 | convolution fusion | flops 1143472000 | bytes 13148672 | tf_op jit(solution)/shard_map/dot_general | solution.py:420
  49.7 0.9 fusion.7.kernel_ref
  50.6 0.2 fusion.8
  50.8 1.5 %convolution_convert_fusion = bf16[256,2048]{1,0:T(8,128)(2,1)} fusion(s32[128]{0:T(128)S(1)} %fusion.23, f32[128,2048]{1,0:T(8,128)S(1)} %get-tuple-element.12, f32[2048]{0:T(1024)S(1)} %copy-done.4, f32[128]{0:T(128)S(1)} %add_rsqrt_fusion), kind=kOutput, calls=%fused_computation | convolution fusion | flops 135561216 | bytes 2106368 | tf_op jit(solution)/shard_map/ts,td->sd/dot_general | solution.py:437
  52.4 0.6 fusion.21.hot_ref
  53.0 68.3 %expert_layer.1 = (bf16[16,16,2048]{2,1,0:T(8,128)(2,1)}, f32[1,128]{1,0:T(1,128)}) custom-call(bf16[16,16,2048]{2,1,0:T(8,128)(2,1)} %bitcast.59, f32[16,128]{1,0:T(8,128)} %fusion.7.kernel_ref, f32[16,128]{1,0:T(8,128)} %fusion.21.hot_ref, bf16[704,2048]{1,0:T(8,128)(2,1)} %bitcast.60, bf16[704,2048]{1,0:T(8,128)(2,1)} %bitcast.61, bf16[704,2048]{1,0:T(8,128)(2,1)} %bitcast.62), custom_call_target="tpu_custom_call" | custom-call | tf_op jit(solution)/shard_map/expert_layer/pallas_call | solution.py:346
  121.2 2.4 %fusion.5 = bf16[128,2048]{1,0:T(8,128)(2,1)} fusion(f32[128,2048]{1,0:T(8,128)S(1)} %get-tuple-element.12, bf16[256,2048]{1,0:T(8,128)(2,1)} %bitcast.64, f32[128]{0:T(128)} %bitcast.66, s32[128]{0:T(128)S(1)} %fusion.23), kind=kOutput, calls=%fused_computation.9 | convolution fusion | flops 135036928 | bytes 2622464 | tf_op jit(solution)/shard_map/dot_general | solution.py:443
  123.6 0.5 copy.32
  (23 shorter events, 0.3 us)
Async XLA Ops:
  0.6 49.1 %copy-start = (bf16[2048,16]{0,1:T(8,128)(2,1)S(1)}, bf16[2048,16]{0,1:T(8,128)(2,1)}, u32[]{:S(2)}) copy-start(bf16[2048,16]{0,1:T(8,128)(2,1)} %param.21) | copy-start | bytes 196612
  0.6 2.6 %copy-start.3 = (bf16[128,128]{1,0:T(8,128)(2,1)S(1)}, bf16[128,128]{1,0:T(8,128)(2,1)}, u32[]{:S(2)}) copy-start(bf16[128,128]{1,0:T(8,128)(2,1)} %param.15) | copy-start | bytes 98308
  1.8 39.8 %copy-start.2 = (bf16[128,128]{1,0:T(8,128)(2,1)S(1)}, bf16[128,128]{1,0:T(8,128)(2,1)}, u32[]{:S(2)}) copy-start(bf16[128,128]{1,0:T(8,128)(2,1)} %param.16) | copy-start | bytes 98308
  41.8 2.1 %copy-start.6 = (f32[32]{0:T(128)S(1)}, f32[32]{0:T(128)}, u32[]{:S(2)}) copy-start(f32[32]{0:T(128)} %param.18) | copy-start | bytes 388
  41.8 2.3 %copy-start.1 = (bf16[128,2048]{1,0:T(8,128)(2,1)S(1)}, bf16[128,2048]{1,0:T(8,128)(2,1)}, u32[]{:S(2)}) copy-start(bf16[128,2048]{1,0:T(8,128)(2,1)} %entry_states.1) | copy-start | bytes 1572868
  44.1 5.6 %copy-start.4 = (f32[2048]{0:T(1024)S(1)}, f32[2048]{0:T(1024)}, u32[]{:S(2)}) copy-start(f32[2048]{0:T(1024)} %param.20) | copy-start | bytes 24580
  44.1 6.6 %copy-start.7 = (s32[128,1]{0,1:T(1,128)S(1)}, s32[128,1]{0,1:T(1,128)}, u32[]{:S(2)}) copy-start(s32[128,1]{0,1:T(1,128)} %param.22) | copy-start | bytes 1540
  121.2 2.4 %copy-start.5 = (f32[1,128]{1,0:T(1,128)S(1)}, f32[1,128]{1,0:T(1,128)}, u32[]{:S(2)}) copy-start(f32[1,128]{1,0:T(1,128)} %get-tuple-element.4) | copy-start | bytes 1540

commit v4 on v3

--- a/solution.py
+++ b/solution.py
@@ -146,7 +146,9 @@
             held, held, pltpu.VMEM((devices, 1, LANES), jnp.float32),
             each, each, dma((devices,)), dma((devices,)), each, each, dma((1 + pieces,)),
         ],
-        compiler_params=pltpu.CompilerParams(collective_id=0, has_side_effects=True),
+        compiler_params=pltpu.CompilerParams(
+            collective_id=0, has_side_effects=True, vmem_limit_bytes=16 << 20
+        ),
         name="entry_states",
     )(block_state.astype(jnp.bfloat16), factor.reshape(groups, 1, LANES))
 
@@ -335,7 +337,7 @@
     lines, spots = lax.axis_size("seq"), lax.axis_size("exp")
     experts, capacity, width = packed.shape
     hidden_units = down_half.shape[0]
-    group = 4
+    group = 8
     dma = pltpu.SemaphoreType.DMA
     vmem = pl.BlockSpec(memory_space=pltpu.VMEM)
     anywhere = pl.BlockSpec(memory_space=pl.ANY)

time: 124 us -> 120 us (0.968)
  Pallas kernels: 104 us -> 101 us
    pallas_call x1, Pallas kernels: 36.2 us -> 34.3 us  [entering(): pl.pallas_call(functools.partial(entry_kernel, devices, pieces), out_shap...]
    pallas_call x1, Pallas kernels: 68.3 us -> 67 us  [expert_layer(): pl.pallas_call(functools.partial(expert_kernel, devices, group), out_shap...]
    unnamed x19 -> x17, local copies, waits for them, and re-layouts: 2.74 us -> 2.74 us
where the time goes in v4:
time: 120 us
  Pallas kernels  101 us (84%)
  matrix products  13 us (11%)
  local copies, waits for them, and re-layouts  3.48 us (3%)
    pallas_call x1, Pallas kernels, expert_layer(): pl.pallas_call(functools.partial(expert_kernel, devices, group), out_shap...  67 us
    pallas_call x1, Pallas kernels, entering(): pl.pallas_call(functools.partial(entry_kernel, devices, pieces), out_shap...  34.3 us
    dot_general x1, matrix products, per_device(): jnp.dot(scan_out, out_proj, preferred_element_type=jnp.float32)  5.6 us
    unnamed x17, local copies, waits for them, and re-layouts  2.74 us

profile of v4, /device:TPU:1, one launch (start us, length us, event | category | flops | bytes accessed | tf_op | source)
XLA Modules:
  0.0 119.6 jit_solution(12502151416113485981)
XLA Ops:
  0.7 0.8 copy.22
  1.5 0.2 reduce_window_sum.11
  1.7 0.1 exponential_multiply_fusion
  1.8 1.3 %copy.27 = bf16[128,2048]{0,1:T(8,128)(2,1)S(1)} copy(bf16[128,2048]{1,0:T(8,128)(2,1)} %param.14) | data formatting | bytes 1048576 | tf_op args[1]
  3.2 0.1 fusion.10
  3.3 0.3 fusion.6.src_ref
  3.7 0.1 exp.25
  3.7 0.1 broadcast_in_dim.19
  3.8 0.1 broadcast_in_dim.20.factor_ref
  3.9 34.3 %entry_states.1 = bf16[128,2048]{1,0:T(8,128)(2,1)S(1)} custom-call(bf16[128,2048]{1,0:T(8,128)(2,1)S(1)} %fusion.6.src_ref, f32[16,1,128]{2,1,0:T(1,128)S(1)} %broadcast_in_dim.20.factor_ref), custom_call_target="tpu_custom_call" | custom-call | tf_op jit(solution)/shard_map/entry_states/pallas_call | solution.py:140
  38.3 0.1 copy.23
  38.4 0.2 fusion.25
  38.6 1.9 %fusion.9 = f32[32,128,64]{1,2,0:T(8,128)} fusion(bf16[128,32,64]{0,2,1:T(8,128)(2,1)S(1)} %bitcast.57, f32[128,128]{1,0:T(8,128)S(1)} %fusion.25, f32[32,128]{1,0:T(8,128)S(1)} %copy.26, f32[32,128]{1,0:T(8,128)S(1)} %copy.23, pred[128,128]{1,0:T(8,128)(4,1)S(1)} %iota_compare_fusion.3), kind=kOutput, calls=%fused_computation.19 | convolution fusion | flops 70254592 | bytes 1687552 | tf_op jit(solution)/shard_map/hts,shp->thp/dot_general | solution.py:389
  40.6 0.1 broadcast_in_dim.17
  40.7 0.1 broadcast_in_dim.38
  40.8 0.1 mul.89
  40.8 5.6 %multiply_reduce_fusion = (f32[128]{0:T(128)S(1)}, f32[128,2048]{1,0:T(8,128)S(1)}) fusion(bf16[2048,2048]{1,0:T(8,128)(2,1)} %param.19, f32[128,2048]{0,1:T(8,128)} %bitcast.63, f32[128,2048]{0,1:T(8,128)S(1)} %bitcast.58, bf16[128,2048]{1,0:T(8,128)(2,1)S(1)} %entry_states.1, bf16[128,128]{1,0:T(8,128)(2,1)S(1)} %copy-done.1, ...), kind=kOutput, calls=%fused_computation.22 | convolution fusion | flops 1143472000 | bytes 13148672 | tf_op jit(solution)/shard_map/dot_general | solution.py:422
  46.5 0.9 fusion.7.kernel_ref
  47.4 0.2 fusion.8
  47.6 1.5 %convolution_convert_fusion = bf16[256,2048]{1,0:T(8,128)(2,1)} fusion(s32[128]{0:T(128)S(1)} %fusion.23, f32[128,2048]{1,0:T(8,128)S(1)} %get-tuple-element.12, f32[2048]{0:T(1024)S(1)} %copy-done.3, f32[128]{0:T(128)S(1)} %add_rsqrt_fusion), kind=kOutput, calls=%fused_computation | convolution fusion | flops 135561216 | bytes 2106368 | tf_op jit(solution)/shard_map/ts,td->sd/dot_general | solution.py:439
  49.1 0.6 fusion.21.hot_ref
  49.7 67.0 %expert_layer.1 = (bf16[16,16,2048]{2,1,0:T(8,128)(2,1)}, f32[1,128]{1,0:T(1,128)}) custom-call(bf16[16,16,2048]{2,1,0:T(8,128)(2,1)} %bitcast.59, f32[16,128]{1,0:T(8,128)} %fusion.7.kernel_ref, f32[16,128]{1,0:T(8,128)} %fusion.21.hot_ref, bf16[704,2048]{1,0:T(8,128)(2,1)} %bitcast.60, bf16[704,2048]{1,0:T(8,128)(2,1)} %bitcast.61, bf16[704,2048]{1,0:T(8,128)(2,1)} %bitcast.62), custom_call_target="tpu_custom_call" | custom-call | tf_op jit(solution)/shard_map/expert_layer/pallas_call | solution.py:348
  116.7 2.4 %fusion.5 = bf16[128,2048]{1,0:T(8,128)(2,1)} fusion(f32[128,2048]{1,0:T(8,128)S(1)} %get-tuple-element.12, bf16[256,2048]{1,0:T(8,128)(2,1)} %bitcast.64, f32[128]{0:T(128)} %bitcast.66, s32[128]{0:T(128)S(1)} %fusion.23), kind=kOutput, calls=%fused_computation.9 | convolution fusion | flops 135036928 | bytes 2622464 | tf_op jit(solution)/shard_map/dot_general | solution.py:445
  119.1 0.5 copy.32
  (21 shorter events, 0.3 us)
Async XLA Ops:
  0.6 45.8 %copy-start = (bf16[2048,16]{0,1:T(8,128)(2,1)S(1)}, bf16[2048,16]{0,1:T(8,128)(2,1)}, u32[]{:S(2)}) copy-start(bf16[2048,16]{0,1:T(8,128)(2,1)} %param.21) | copy-start | bytes 196612
  0.6 2.6 %copy-start.2 = (bf16[128,128]{1,0:T(8,128)(2,1)S(1)}, bf16[128,128]{1,0:T(8,128)(2,1)}, u32[]{:S(2)}) copy-start(bf16[128,128]{1,0:T(8,128)(2,1)} %param.15) | copy-start | bytes 98308
  1.8 36.6 %copy-start.1 = (bf16[128,128]{1,0:T(8,128)(2,1)S(1)}, bf16[128,128]{1,0:T(8,128)(2,1)}, u32[]{:S(2)}) copy-start(bf16[128,128]{1,0:T(8,128)(2,1)} %param.16) | copy-start | bytes 98308
  38.6 2.1 %copy-start.5 = (f32[32]{0:T(128)S(1)}, f32[32]{0:T(128)}, u32[]{:S(2)}) copy-start(f32[32]{0:T(128)} %param.18) | copy-start | bytes 388
  40.8 5.6 %copy-start.3 = (f32[2048]{0:T(1024)S(1)}, f32[2048]{0:T(1024)}, u32[]{:S(2)}) copy-start(f32[2048]{0:T(1024)} %param.20) | copy-start | bytes 24580
  40.8 6.6 %copy-start.6 = (s32[128,1]{0,1:T(1,128)S(1)}, s32[128,1]{0,1:T(1,128)}, u32[]{:S(2)}) copy-start(s32[128,1]{0,1:T(1,128)} %param.22) | copy-start | bytes 1540
  116.7 2.4 %copy-start.4 = (f32[1,128]{1,0:T(1,128)S(1)}, f32[1,128]{1,0:T(1,128)}, u32[]{:S(2)}) copy-start(f32[1,128]{1,0:T(1,128)} %get-tuple-element.4) | copy-start | bytes 1540

commit v5 on v4

--- a/solution.py
+++ b/solution.py
@@ -360,7 +360,10 @@
             each, each, each, each, each, each, each, each,
             dma((spots,)), dma((spots,)), dma((lines,)), dma((lines,)), dma((2,)), dma((3,)),
         ],
-        compiler_params=pltpu.CompilerParams(collective_id=1, has_side_effects=True),
+        compiler_params=pltpu.CompilerParams(
+            collective_id=1, has_side_effects=True,
+            vmem_limit_bytes=(20 << 20) + 20 * experts * capacity * width
+        ),
         name="expert_layer",
     )(packed, kernel, hot, gate_half.T, up_half.T, down_half)
 

time: 120 us -> 122 us (1.017)
  local copies, waits for them, and re-layouts: 3.48 us -> 6.32 us
  matrix products: 13 us -> 14.3 us
  Pallas kernels: 101 us -> 99.7 us
    unnamed x17 -> x25, local copies, waits for them, and re-layouts: 2.74 us -> 4.56 us
    pallas_call x1, Pallas kernels: 67 us -> 65.3 us  [expert_layer(): pl.pallas_call(functools.partial(expert_kernel, devices, group), out_shap...]
    dot_general x1, matrix products: 5.6 us -> 7.1 us  [per_device(): jnp.dot(scan_out, out_proj, preferred_element_type=jnp.float32)]
    dot_general x1, matrix products: 2.38 us -> 1.15 us  [per_device(): jnp.dot(spread, summed.reshape(experts * capacity, model_width), preferre...]
where the time goes in v5:
time: 122 us
  Pallas kernels  99.7 us (82%)
  matrix products  14.3 us (12%)
  local copies, waits for them, and re-layouts  6.32 us (5%)
    pallas_call x1, Pallas kernels, expert_layer(): pl.pallas_call(functools.partial(expert_kernel, devices, group), out_shap...  65.3 us
    pallas_call x1, Pallas kernels, entering(): pl.pallas_call(functools.partial(entry_kernel, devices, pieces), out_shap...  34.3 us
    dot_general x1, matrix products, per_device(): jnp.dot(scan_out, out_proj, preferred_element_type=jnp.float32)  7.1 us
    unnamed x25, local copies, waits for them, and re-layouts  4.56 us

profile of v5, /device:TPU:1, one launch (start us, length us, event | category | flops | bytes accessed | tf_op | source)
XLA Modules:
  0.0 121.5 jit_solution(14767242179785086235)
XLA Ops:
  0.7 0.8 copy.22
  1.5 0.2 reduce_window_sum.11
  1.7 0.1 exponential_multiply_fusion
  1.8 1.3 %copy.27 = bf16[128,2048]{0,1:T(8,128)(2,1)S(1)} copy(bf16[128,2048]{1,0:T(8,128)(2,1)} %param.14) | data formatting | bytes 1048576 | tf_op args[1]
  3.2 0.1 fusion.10
  3.3 0.3 fusion.6.src_ref
  3.7 0.1 exp.25
  3.7 0.1 broadcast_in_dim.19
  3.8 0.1 broadcast_in_dim.20.factor_ref
  3.9 34.3 %entry_states.1 = bf16[128,2048]{1,0:T(8,128)(2,1)S(1)} custom-call(bf16[128,2048]{1,0:T(8,128)(2,1)S(1)} %fusion.6.src_ref, f32[16,1,128]{2,1,0:T(1,128)S(1)} %broadcast_in_dim.20.factor_ref), custom_call_target="tpu_custom_call" | custom-call | tf_op jit(solution)/shard_map/entry_states/pallas_call | solution.py:140
  38.3 0.1 copy.23
  38.4 0.2 fusion.25
  38.6 1.9 %fusion.9 = f32[32,128,64]{1,2,0:T(8,128)} fusion(bf16[128,32,64]{0,2,1:T(8,128)(2,1)S(1)} %bitcast.64, f32[128,128]{1,0:T(8,128)S(1)} %fusion.25, f32[32,128]{1,0:T(8,128)S(1)} %copy.26, f32[32,128]{1,0:T(8,128)S(1)} %copy.23, pred[128,128]{1,0:T(8,128)(4,1)S(1)} %iota_compare_fusion.3), kind=kOutput, calls=%fused_computation.19 | convolution fusion | flops 70254592 | bytes 1687552 | tf_op jit(solution)/shard_map/hts,shp->thp/dot_general | solution.py:392
  40.6 1.1 broadcast_in_dim.17
  41.7 0.1 broadcast_in_dim.38
  41.8 0.1 mul.89
  41.8 7.1 %multiply_reduce_fusion = (f32[128]{0:T(128)S(1)}, f32[128,2048]{1,0:T(8,128)}) fusion(bf16[2048,2048]{1,0:T(8,128)(2,1)} %param.19, f32[128,2048]{0,1:T(8,128)} %bitcast.66, f32[128,2048]{0,1:T(8,128)} %bitcast.65, bf16[128,2048]{1,0:T(8,128)(2,1)S(1)} %entry_states.1, bf16[128,128]{1,0:T(8,128)(2,1)S(1)} %copy-done.6, bf16[128,2048]{0,1:T(8,128)(2,1)} %copy-done.5, ...), kind=kOutput, calls=%fused_computation.22 | convolution fusion | flops 1143472000 | bytes 13148672 | tf_op jit(solution)/shard_map/dot_general | solution.py:425
  49.0 1.7 %fusion.7.kernel_ref = f32[16,128]{1,0:T(8,128)S(1)} fusion(bf16[2048,16]{0,1:T(8,128)(2,1)S(1)} %copy-done, f32[128,2048]{1,0:T(8,128)} %get-tuple-element.12, f32[2048]{0:T(1024)S(1)} %copy-done.8, f32[128]{0:T(128)S(1)} %add_rsqrt_fusion), kind=kOutput, calls=%fused_computation.17 | convolution fusion | flops 9175040 | bytes 1131008 | tf_op jit(solution)/shard_map/de,td->et/dot_general | solution.py:430
  50.7 0.2 fusion.8
  50.9 1.8 %convolution_convert_fusion = bf16[256,2048]{1,0:T(8,128)(2,1)S(1)} fusion(s32[128]{0:T(128)S(1)} %fusion.23, f32[128,2048]{1,0:T(8,128)} %get-tuple-element.12, f32[2048]{0:T(1024)S(1)} %copy-done.8, f32[128]{0:T(128)S(1)} %add_rsqrt_fusion), kind=kOutput, calls=%fused_computation | convolution fusion | flops 135561216 | bytes 2106368 | tf_op jit(solution)/shard_map/ts,td->sd/dot_general | solution.py:442
  52.7 1.8 %copy-done.3 = bf16[1,704,2048]{2,1,0:T(8,128)(2,1)S(1)} copy-done((bf16[1,704,2048]{2,1,0:T(8,128)(2,1)S(1)}, bf16[1,704,2048]{2,1,0:T(8,128)(2,1)}, u32[]{:S(2)}) %copy-start.3) | copy-done | bytes 2883608
  54.5 65.3 %expert_layer.1 = (bf16[16,16,2048]{2,1,0:T(8,128)(2,1)S(1)}, f32[1,128]{1,0:T(1,128)S(1)}) custom-call(bf16[16,16,2048]{2,1,0:T(8,128)(2,1)S(1)} %bitcast.57, f32[16,128]{1,0:T(8,128)S(1)} %fusion.7.kernel_ref, f32[16,128]{1,0:T(8,128)S(1)} %fusion.21.hot_ref, bf16[704,2048]{1,0:T(8,128)(2,1)S(1)} %bitcast.58, bf16[704,2048]{1,0:T(8,128)(2,1)S(1)} %bitcast.59, ...), custom_call_target="tpu_custom_call" | custom-call | tf_op jit(solution)/shard_map/expert_layer/pallas_call | solution.py:348
  119.9 1.1 fusion.5
  121.0 0.5 copy.32
  (29 shorter events, 0.3 us)
Async XLA Ops:
  0.6 48.3 %copy-start = (bf16[2048,16]{0,1:T(8,128)(2,1)S(1)}, bf16[2048,16]{0,1:T(8,128)(2,1)}, u32[]{:S(2)}) copy-start(bf16[2048,16]{0,1:T(8,128)(2,1)} %param.21) | copy-start | bytes 196612
  0.6 2.7 %copy-start.7 = (bf16[128,128]{1,0:T(8,128)(2,1)S(1)}, bf16[128,128]{1,0:T(8,128)(2,1)}, u32[]{:S(2)}) copy-start(bf16[128,128]{1,0:T(8,128)(2,1)} %param.15) | copy-start | bytes 98308
  1.8 36.6 %copy-start.6 = (bf16[128,128]{1,0:T(8,128)(2,1)S(1)}, bf16[128,128]{1,0:T(8,128)(2,1)}, u32[]{:S(2)}) copy-start(bf16[128,128]{1,0:T(8,128)(2,1)} %param.16) | copy-start | bytes 98308
  3.2 37.4 %copy-start.5 = (bf16[128,2048]{0,1:T(8,128)(2,1)}, bf16[128,2048]{0,1:T(8,128)(2,1)S(1)}, u32[]{:S(2)}) copy-start(bf16[128,2048]{0,1:T(8,128)(2,1)S(1)} %copy.27) | copy-start | bytes 1572868
  38.6 3.1 %copy-start.9 = (f32[32]{0:T(128)S(1)}, f32[32]{0:T(128)}, u32[]{:S(2)}) copy-start(f32[32]{0:T(128)} %param.18) | copy-start | bytes 388
  41.8 7.1 %copy-start.8 = (f32[2048]{0:T(1024)S(1)}, f32[2048]{0:T(1024)}, u32[]{:S(2)}) copy-start(f32[2048]{0:T(1024)} %param.20) | copy-start | bytes 24580
  41.8 8.8 %copy-start.10 = (s32[128,1]{0,1:T(1,128)S(1)}, s32[128,1]{0,1:T(1,128)}, u32[]{:S(2)}) copy-start(s32[128,1]{0,1:T(1,128)} %param.22) | copy-start | bytes 1540
  41.8 10.8 %copy-start.2 = (bf16[1,2048,704]{1,2,0:T(8,128)(2,1)S(1)}, bf16[1,2048,704]{1,2,0:T(8,128)(2,1)}, u32[]{:S(2)}) copy-start(bf16[1,2048,704]{1,2,0:T(8,128)(2,1)} %param.24) | copy-start | bytes 8650756
  48.9 3.7 %copy-start.1 = (bf16[1,2048,704]{1,2,0:T(8,128)(2,1)S(1)}, bf16[1,2048,704]{1,2,0:T(8,128)(2,1)}, u32[]{:S(2)}) copy-start(bf16[1,2048,704]{1,2,0:T(8,128)(2,1)} %param.23) | copy-start | bytes 8650756
  52.7 1.8 %copy-start.3 = (bf16[1,704,2048]{2,1,0:T(8,128)(2,1)S(1)}, bf16[1,704,2048]{2,1,0:T(8,128)(2,1)}, u32[]{:S(2)}) copy-start(bf16[1,704,2048]{2,1,0:T(8,128)(2,1)} %param.25) | copy-start | bytes 8650756
  54.5 65.4 %copy-start.4 = (f32[128,2048]{1,0:T(8,128)S(1)}, f32[128,2048]{1,0:T(8,128)}, u32[]{:S(2)}) copy-start(f32[128,2048]{1,0:T(8,128)} %get-tuple-element.12) | copy-start | bytes 3145732
